TPU v7x, 32 devices: a whole 2x2x4 slice. The times are simulated.
32 devices in a mesh: dp: 4 (over z), seq: 4 (over y, x), mp: 2 (over core).
Axes of the slice: x: 2, y: 2, z: 4, core: 2. Of those that a mesh axis runs over, the one named last changes fastest.
Arguments:
- tokens: bfloat16 [8, 1024, 768], P('dp', 'seq'), may hold values from -6 to 6
- segments: int32 [8, 1024], P('dp'), may hold values from 0 to 3, as said below
- dropped: int32 [8], replicated, may hold values from 0 to 1, as said below
- qkv_weight: bfloat16 [2, 3, 768, 768], P(None, None, None, 'mp'), may hold values from -0.21875 to 0.21875
- qv_bias: float32 [2, 2, 768], P(None, None, 'mp'), may hold values from -3 to 3
- out_weight: bfloat16 [2, 768, 768], P(None, 'mp'), may hold values from -1.5 to 1.5
- out_bias: float32 [2, 768], replicated, may hold values from -2 to 2
- norm_gain: float32 [2, 2, 768], replicated, may hold values from 0.5 to 1.5
- norm_shift: float32 [2, 2, 768], replicated, may hold values from -1.5 to 1.5
- up_weight: bfloat16 [2, 768, 3072], P(None, None, 'mp'), may hold values from -0.21875 to 0.21875
- up_bias: float32 [2, 3072], P(None, 'mp'), may hold values from -3 to 3
- down_weight: bfloat16 [2, 3072, 768], P(None, 'mp'), may hold values from -0.109375 to 0.109375
- down_bias: float32 [2, 768], replicated, may hold values from -2 to 2
- cotangent: bfloat16 [8, 1024, 768], P('dp', 'seq'), may hold values from -6 to 6
Outputs:
- outputs: float32 [8, 1024, 768], P('dp', 'seq')
- tokens_grad: float32 [8, 1024, 768], P('dp', 'seq')
- qkv_grad: float32 [2, 3, 768, 768], P(None, None, 'dp', 'mp')
- qv_bias_grad: float32 [2, 2, 768], P(None, None, 'mp')
- out_grad: float32 [2, 768, 768], P(None, 'mp', 'dp')
- out_bias_grad: float32 [2, 768], replicated
- gain_grad: float32 [2, 2, 768], replicated
- shift_grad: float32 [2, 2, 768], replicated
- up_grad: float32 [2, 768, 3072], P(None, 'dp', 'mp')
- up_bias_grad: float32 [2, 3072], P(None, 'mp')
- down_grad: float32 [2, 3072, 768], P(None, 'mp', 'dp')
- down_bias_grad: float32 [2, 768], replicated
Inputs may be any that keep to these rules, and one draw needn't show every extreme that they name: `dropped`: exactly 1 row have 1. `segments`: within a row the ids never fall and every id appears.
All inputs are finite; a program needn't handle non-finite values.
Results may differ from a plain program's by a relative error of at most 0.033.
Values may be sent and summed in bfloat16 or wider, within the bound.
No kernel may reach another device: no remote copies, remote signals or barrier semaphores. Data moves between devices by JAX's collectives and lax.ppermute only.
A program may use at most 128 MiB of HBM per device.

v0:
```python
import jax
import jax.numpy as jnp
from jax import lax
from jax.sharding import PartitionSpec as P

HEAD = 64


eps_norm = 1e-05
root_half = 0.7071067811865476
inv_root_tau = 0.3989422804014327


def dot_float(left, right):
    return jnp.dot(left, right, preferred_element_type=jnp.float32)


def head_total(partial_sum):
    return lax.psum(partial_sum.astype(jnp.bfloat16), "mp").astype(jnp.float32)


def normalize(rows_in, gain, shift):
    center = rows_in - jnp.mean(rows_in, axis=-1, keepdims=True)
    scale = lax.rsqrt(jnp.mean(center * center, axis=-1, keepdims=True) + eps_norm)
    unit = center * scale
    return (unit * gain + shift, unit, scale)


def normalize_back(grad_out, unit, scale, gain):
    grad_unit = grad_out * gain
    inner = (
        grad_unit
        - jnp.mean(grad_unit, axis=-1, keepdims=True)
        - unit * jnp.mean(grad_unit * unit, axis=-1, keepdims=True)
    )
    return (inner * scale, jnp.sum(grad_out * unit, axis=0), jnp.sum(grad_out, axis=0))


def attend_rows(query, key_all, value_all, same):

    def one_row(item):
        query_row, key_row, value_row, mask_row = item
        scores = (
            jnp.einsum("qhd,khd->hqk", query_row, key_row, preferred_element_type=jnp.float32)
            * 0.125
        )
        scores = jnp.where(mask_row[None], scores, -1e30)
        peak = jnp.max(scores, axis=-1, keepdims=True)
        raised = jnp.exp(scores - peak)
        total = jnp.sum(raised, axis=-1, keepdims=True)
        weights = (raised / total).astype(jnp.bfloat16)
        context = jnp.einsum("hqk,khd->qhd", weights, value_row, preferred_element_type=jnp.float32)
        return (context.astype(jnp.bfloat16), peak[..., 0] + jnp.log(total[..., 0]))

    return lax.map(one_row, (query, key_all, value_all, same))


def attend_back(query, key_all, value_all, same, log_total, grad_context):

    def one_row(item):
        query_row, key_row, value_row, mask_row, total_row, grad_row = item
        scores = (
            jnp.einsum("qhd,khd->hqk", query_row, key_row, preferred_element_type=jnp.float32)
            * 0.125
        )
        chance = jnp.where(mask_row[None], jnp.exp(scores - total_row[..., None]), 0.0)
        grad_chance = jnp.einsum(
            "qhd,khd->hqk", grad_row, value_row, preferred_element_type=jnp.float32
        )
        grad_value = jnp.einsum(
            "hqk,qhd->khd",
            chance.astype(jnp.bfloat16),
            grad_row,
            preferred_element_type=jnp.float32,
        )
        grad_score = chance * (grad_chance - jnp.sum(grad_chance * chance, axis=-1, keepdims=True))
        grad_score = grad_score.astype(jnp.bfloat16)
        grad_query = (
            jnp.einsum("hqk,khd->qhd", grad_score, key_row, preferred_element_type=jnp.float32)
            * 0.125
        )
        grad_key = (
            jnp.einsum("hqk,qhd->khd", grad_score, query_row, preferred_element_type=jnp.float32)
            * 0.125
        )
        return (grad_query, grad_key, grad_value)

    return lax.map(one_row, (query, key_all, value_all, same, log_total, grad_context))


def layer_forward(inputs, seg_keys, seg_query, params):
    (
        weight_qkv,
        bias_qv,
        weight_out,
        bias_out,
        gain,
        shift,
        weight_up,
        bias_up,
        weight_down,
        bias_down,
    ) = params
    batch, span, width = inputs.shape
    flat = inputs.reshape(batch * span, width)
    low_in = flat.astype(jnp.bfloat16)
    query = (dot_float(low_in, weight_qkv[0]) + bias_qv[0]).astype(jnp.bfloat16)
    keys = dot_float(low_in, weight_qkv[1]).astype(jnp.bfloat16)
    values = (dot_float(low_in, weight_qkv[2]) + bias_qv[1]).astype(jnp.bfloat16)
    local_width = query.shape[1]
    head_count = local_width // HEAD
    keys = keys.reshape(batch, span, local_width)
    values = values.reshape(batch, span, local_width)
    key_all, value_all = (
        lax.all_gather(keys, "seq", axis=1, tiled=True),
        lax.all_gather(values, "seq", axis=1, tiled=True),
    )
    full = key_all.shape[1]
    query_heads = query.reshape(batch, span, head_count, HEAD)
    same = seg_query[:, :, None] == seg_keys[:, None, :]
    context, log_total = attend_rows(
        query_heads,
        key_all.reshape(batch, full, head_count, HEAD),
        value_all.reshape(batch, full, head_count, HEAD),
        same,
    )
    context_flat = context.reshape(batch * span, local_width)
    out_partial = dot_float(context_flat, weight_out)
    attended = head_total(out_partial) + bias_out
    hidden, unit_one, scale_one = normalize(flat + attended, gain[0], shift[0])
    low_hidden = hidden.astype(jnp.bfloat16)
    pre_act = dot_float(low_hidden, weight_up) + bias_up
    low_act = jax.nn.gelu(pre_act, approximate=False).astype(jnp.bfloat16)
    down_partial = dot_float(low_act, weight_down)
    mixed = head_total(down_partial) + bias_down
    result, unit_two, scale_two = normalize(hidden + mixed, gain[1], shift[1])
    key_store = (keys, values)
    saved = (
        low_in,
        query_heads,
        key_store,
        same,
        log_total,
        context_flat,
        unit_one,
        scale_one,
        low_hidden,
        pre_act,
        low_act,
        unit_two,
        scale_two,
    )
    return (result.reshape(batch, span, width), saved)


def layer_backward(grad_result, saved, params):
    (
        weight_qkv,
        bias_qv,
        weight_out,
        bias_out,
        gain,
        shift,
        weight_up,
        bias_up,
        weight_down,
        bias_down,
    ) = params
    (
        low_in,
        query_heads,
        key_store,
        same,
        log_total,
        context_flat,
        unit_one,
        scale_one,
        low_hidden,
        pre_act,
        low_act,
        unit_two,
        scale_two,
    ) = saved
    batch, span, width = grad_result.shape
    grad_flat = grad_result.reshape(batch * span, width)
    grad_mixed, gain_two, shift_two = normalize_back(grad_flat, unit_two, scale_two, gain[1])
    grad_bias_down = jnp.sum(grad_mixed, axis=0)
    mixed_own = grad_mixed.astype(jnp.bfloat16)
    grad_weight_down = jnp.einsum(
        "nf,nd->fd", low_act, mixed_own, preferred_element_type=jnp.float32
    )
    grad_act = jnp.einsum("nd,fd->nf", mixed_own, weight_down, preferred_element_type=jnp.float32)
    normal_cdf = 0.5 * (1.0 + lax.erf(pre_act * root_half))
    density = jnp.exp(-0.5 * pre_act * pre_act) * inv_root_tau
    low_pre = (grad_act * (normal_cdf + pre_act * density)).astype(jnp.bfloat16)
    grad_bias_up = jnp.sum(low_pre.astype(jnp.float32), axis=0)
    grad_weight_up = jnp.einsum(
        "nd,nf->df", low_hidden, low_pre, preferred_element_type=jnp.float32
    )
    back_ffn = jnp.einsum("nf,df->nd", low_pre, weight_up, preferred_element_type=jnp.float32)
    grad_hidden = grad_mixed + head_total(back_ffn)
    grad_attended, gain_one, shift_one = normalize_back(grad_hidden, unit_one, scale_one, gain[0])
    grad_bias_out = jnp.sum(grad_attended, axis=0)
    attended_own = grad_attended.astype(jnp.bfloat16)
    grad_weight_out = jnp.einsum(
        "nc,nd->cd", context_flat, attended_own, preferred_element_type=jnp.float32
    )
    grad_context = jnp.einsum(
        "nd,cd->nc", attended_own, weight_out, preferred_element_type=jnp.float32
    ).astype(jnp.bfloat16)
    key_all, value_all = (
        lax.all_gather(key_store[0], "seq", axis=1, tiled=True),
        lax.all_gather(key_store[1], "seq", axis=1, tiled=True),
    )
    head_count = query_heads.shape[2]
    local_width = head_count * HEAD
    full = key_all.shape[1]
    grad_query, grad_key, grad_value = attend_back(
        query_heads,
        key_all.reshape(batch, full, head_count, HEAD),
        value_all.reshape(batch, full, head_count, HEAD),
        same,
        log_total,
        grad_context.reshape(batch, span, head_count, HEAD),
    )
    grad_key, grad_value = (
        lax.psum_scatter(
            grad_key.reshape(batch, full, local_width).astype(jnp.bfloat16),
            "seq",
            scatter_dimension=1,
            tiled=True,
        ).astype(jnp.float32),
        lax.psum_scatter(
            grad_value.reshape(batch, full, local_width).astype(jnp.bfloat16),
            "seq",
            scatter_dimension=1,
            tiled=True,
        ).astype(jnp.float32),
    )
    low_query = grad_query.reshape(batch * span, local_width).astype(jnp.bfloat16)
    low_key = grad_key.reshape(batch * span, local_width).astype(jnp.bfloat16)
    low_value = grad_value.reshape(batch * span, local_width).astype(jnp.bfloat16)
    back_qkv = jnp.einsum("nc,dc->nd", low_query, weight_qkv[0], preferred_element_type=jnp.float32)
    back_qkv = back_qkv + jnp.einsum(
        "nc,dc->nd", low_key, weight_qkv[1], preferred_element_type=jnp.float32
    )
    back_qkv = back_qkv + jnp.einsum(
        "nc,dc->nd", low_value, weight_qkv[2], preferred_element_type=jnp.float32
    )
    grad_inputs = grad_attended + head_total(back_qkv)
    grad_weight_qkv = jnp.stack(
        [
            jnp.einsum("nd,nc->dc", low_in, low_query, preferred_element_type=jnp.float32),
            jnp.einsum("nd,nc->dc", low_in, low_key, preferred_element_type=jnp.float32),
            jnp.einsum("nd,nc->dc", low_in, low_value, preferred_element_type=jnp.float32),
        ]
    )
    grad_bias_qv = jnp.stack(
        [
            jnp.sum(low_query.astype(jnp.float32), axis=0),
            jnp.sum(low_value.astype(jnp.float32), axis=0),
        ]
    )
    grads = (
        grad_weight_qkv,
        grad_bias_qv,
        grad_weight_out,
        grad_bias_out,
        jnp.stack([gain_one, gain_two]),
        jnp.stack([shift_one, shift_two]),
        grad_weight_up,
        grad_bias_up,
        grad_weight_down,
        grad_bias_down,
    )
    return (grad_inputs.reshape(batch, span, width), grads)


def layer_part(index, params):
    return tuple((array[index] for array in params))


def stack_pair(first_part, second_part):
    return jnp.stack([first_part, second_part])


def local(
    tokens,
    segments,
    dropped,
    qkv_weight,
    qv_bias,
    out_weight,
    out_bias,
    norm_gain,
    norm_shift,
    up_weight,
    up_bias,
    down_weight,
    down_bias,
    cotangent,
):
    params = (
        qkv_weight,
        qv_bias,
        out_weight,
        out_bias,
        norm_gain,
        norm_shift,
        up_weight,
        up_bias,
        down_weight,
        down_bias,
    )
    first = layer_part(0, params)
    second = layer_part(1, params)
    rows_here, span, width = tokens.shape
    seq_place = lax.axis_index("seq")
    seg_query = lax.dynamic_slice_in_dim(segments, seq_place * span, span, 1)
    hidden_one, saved_one = layer_forward(tokens.astype(jnp.float32), segments, seg_query, first)
    groups = lax.axis_size("dp")
    place = lax.axis_index("dp")
    keep_table = (1 - dropped).reshape(groups, rows_here)
    keep_mine = lax.dynamic_index_in_dim(keep_table, place, 0, keepdims=False)
    kept_mine = keep_mine > 0
    kept_shape = kept_mine.reshape(rows_here, 1, 1)
    cot_float = cotangent.astype(jnp.float32)
    result_two, saved_two = layer_forward(hidden_one, segments, seg_query, second)
    outputs = jnp.where(kept_shape, result_two, hidden_one)
    grad_two = jnp.where(kept_shape, cot_float, 0.0)
    grad_in_two, grads_two = layer_backward(grad_two, saved_two, second)
    grad_hidden_one = jnp.where(kept_shape, grad_in_two, cot_float)
    tokens_grad, grads_one = layer_backward(grad_hidden_one, saved_one, first)
    stacked = jax.tree.map(stack_pair, grads_one, grads_two)
    (
        qkv_part,
        qv_part,
        out_part,
        out_bias_part,
        gain_part,
        shift_part,
        up_part,
        up_bias_part,
        down_part,
        down_bias_part,
    ) = stacked
    qkv_share, out_share, up_share, down_share = (
        lax.psum_scatter(
            qkv_part.astype(jnp.bfloat16), "dp", scatter_dimension=2, tiled=True
        ).astype(jnp.float32),
        lax.psum_scatter(
            out_part.astype(jnp.bfloat16), "dp", scatter_dimension=2, tiled=True
        ).astype(jnp.float32),
        lax.psum_scatter(
            up_part.astype(jnp.bfloat16), "dp", scatter_dimension=1, tiled=True
        ).astype(jnp.float32),
        lax.psum_scatter(
            down_part.astype(jnp.bfloat16), "dp", scatter_dimension=2, tiled=True
        ).astype(jnp.float32),
    )
    qkv_sum, out_sum, up_sum, down_sum = (
        lax.psum(qkv_share.astype(jnp.bfloat16), "seq").astype(jnp.float32),
        lax.psum(out_share.astype(jnp.bfloat16), "seq").astype(jnp.float32),
        lax.psum(up_share.astype(jnp.bfloat16), "seq").astype(jnp.float32),
        lax.psum(down_share.astype(jnp.bfloat16), "seq").astype(jnp.float32),
    )
    qv_sum, out_bias_sum, gain_sum, shift_sum, up_bias_sum, down_bias_sum = lax.psum(
        (qv_part, out_bias_part, gain_part, shift_part, up_bias_part, down_bias_part), ("dp", "seq")
    )
    return (
        outputs,
        tokens_grad,
        qkv_sum,
        qv_sum,
        out_sum,
        out_bias_sum,
        gain_sum,
        shift_sum,
        up_sum,
        up_bias_sum,
        down_sum,
        down_bias_sum,
    )


def solution(mesh):
    placed = (
        P("dp", "seq", None),
        P("dp", None),
        P(),
        P(None, None, None, "mp"),
        P(None, None, "mp"),
        P(None, "mp", None),
        P(),
        P(),
        P(),
        P(None, None, "mp"),
        P(None, "mp"),
        P(None, "mp", None),
        P(),
        P("dp", "seq", None),
    )
    return jax.shard_map(
        local,
        mesh=mesh,
        in_specs=placed,
        out_specs=(
            P("dp", "seq", None),
            P("dp", "seq", None),
            P(None, None, "dp", "mp"),
            P(None, None, "mp"),
            P(None, "mp", "dp"),
            P(),
            P(),
            P(),
            P(None, "dp", "mp"),
            P(None, "mp"),
            P(None, "mp", "dp"),
            P(),
        ),
        check_vma=False,
    )
```

profile of v0, /device:TPU:0, one launch (start us, length us, event | category | flops | bytes accessed | tf_op | source)
XLA Modules:
  0.0 1149.2 jit_solution(3419628556144833229)
XLA Ops:
  15.6 28.9 %all-gather.5.cloned.1.call-done = bf16[2,1024,384]{2,1,0:T(8,128)(2,1)} async-done(((bf16[2,256,384]{2,1,0:T(8,128)(2,1)}), bf16[2,1024,384]{2,1,0:T(8,128)(2,1)}) %all-gather.5.cloned.1.call-update) | async-done | bytes 1572880 | tf_op jit(solution)/shard_map/all_gather | solution.py:116
  47.1 30.8 %all-gather.7.cloned.1.call-done = bf16[2,1024,384]{2,1,0:T(8,128)(2,1)} async-done(((bf16[2,256,384]{2,1,0:T(8,128)(2,1)}), bf16[2,1024,384]{2,1,0:T(8,128)(2,1)}) %all-gather.7.cloned.1.call-update) | async-done | bytes 1572880 | tf_op jit(solution)/shard_map/all_gather | solution.py:115
  80.5 11.4 while.52
  97.6 18.9 %all-reduce.17.cloned.1.call-done = bf16[512,768]{1,0:T(8,128)(2,1)} async-done(((bf16[512,768]{1,0:T(8,128)(2,1)}), bf16[512,768]{1,0:T(8,128)(2,1)}) %all-reduce.17.cloned.1.call-update) | async-done | bytes 786448 | tf_op jit(solution)/shard_map/psum | solution.py:19
  120.2 10.9 fusion.98
  134.7 20.5 %all-reduce.19.cloned.1.call-done = bf16[512,768]{1,0:T(8,128)(2,1)} async-done(((bf16[512,768]{1,0:T(8,128)(2,1)}), bf16[512,768]{1,0:T(8,128)(2,1)}) %all-reduce.19.cloned.1.call-update) | async-done | bytes 786448 | tf_op jit(solution)/shard_map/psum | solution.py:19
  166.0 27.6 %all-gather.9.cloned.1.call-done = bf16[2,1024,384]{2,1,0:T(8,128)(2,1)} async-done(((bf16[2,256,384]{2,1,0:T(8,128)(2,1)}), bf16[2,1024,384]{2,1,0:T(8,128)(2,1)}) %all-gather.9.cloned.1.call-update) | async-done | bytes 1572880 | tf_op jit(solution)/shard_map/all_gather | solution.py:116
  196.1 30.7 %all-gather.11.cloned.1.call-done = bf16[2,1024,384]{2,1,0:T(8,128)(2,1)} async-done(((bf16[2,256,384]{2,1,0:T(8,128)(2,1)}), bf16[2,1024,384]{2,1,0:T(8,128)(2,1)}) %all-gather.11.cloned.1.call-update) | async-done | bytes 1572880 | tf_op jit(solution)/shard_map/all_gather | solution.py:115
  228.6 9.6 while.53
  242.6 18.8 %all-reduce.21.cloned.1.call-done = bf16[512,768]{1,0:T(8,128)(2,1)} async-done(((bf16[512,768]{1,0:T(8,128)(2,1)}), bf16[512,768]{1,0:T(8,128)(2,1)}) %all-reduce.21.cloned.1.call-update) | async-done | bytes 786448 | tf_op jit(solution)/shard_map/psum | solution.py:19
  263.8 11.4 fusion.101
  281.1 18.3 %all-reduce.23.cloned.1.call-done = bf16[512,768]{1,0:T(8,128)(2,1)} async-done(((bf16[512,768]{1,0:T(8,128)(2,1)}), bf16[512,768]{1,0:T(8,128)(2,1)}) %all-reduce.23.cloned.1.call-update) | async-done | bytes 786448 | tf_op jit(solution)/shard_map/psum | solution.py:19
  305.0 3.2 convert_reduce_fusion
  312.0 20.4 %all-reduce.25.cloned.1.call-done = bf16[512,768]{1,0:T(8,128)(2,1)} async-done(((bf16[512,768]{1,0:T(8,128)(2,1)}), bf16[512,768]{1,0:T(8,128)(2,1)}) %all-reduce.25.cloned.1.call-update) | async-done | bytes 786448 | tf_op jit(solution)/shard_map/psum | solution.py:19
  332.4 3.7 multiply_reduce_fusion.2
  342.2 20.1 %while.54 = (s32[]{:T(128)}, bf16[2,256,6,64]{1,3,2,0:T(8,128)(2,1)S(1)}, bf16[2,1024,6,64]{1,3,2,0:T(8,128)(2,1)}, bf16[2,1024,6,64]{1,3,2,0:T(8,128)(2,1)}, bf...) while((s32[]{:T(128)}, ...), condition=%wide.region_27.28_spmd, body=%wide.region_25.27_spmd.sunk | while | flops 1030715904 | bytes 74108104 | solution.py:88
  366.5 28.2 %reduce-scatter.6.cloned.1.call-done = bf16[2,256,384]{1,2,0:T(8,128)(2,1)} async-done(((bf16[2,1024,384]{1,2,0:T(8,128)(2,1)}), bf16[2,256,384]{1,2,0:T(8,128)(2,1)}) %reduce-scatter.6.cloned.1.call-update) | async-done | bytes 393232 | tf_op jit(solution)/shard_map/reduce_scatter | solution.py:227
  398.8 30.0 %reduce-scatter.8.cloned.1.call-done = bf16[2,256,384]{1,2,0:T(8,128)(2,1)} async-done(((bf16[2,1024,384]{1,2,0:T(8,128)(2,1)}), bf16[2,256,384]{1,2,0:T(8,128)(2,1)}) %reduce-scatter.8.cloned.1.call-update) | async-done | bytes 393232 | tf_op jit(solution)/shard_map/reduce_scatter | solution.py:233
  430.1 3.7 add_convert_fusion.1
  434.3 18.9 %all-reduce.27.cloned.1.call-done = bf16[512,768]{1,0:T(8,128)(2,1)} async-done(((bf16[512,768]{1,0:T(8,128)(2,1)}), bf16[512,768]{1,0:T(8,128)(2,1)}) %all-reduce.27.cloned.1.call-update) | async-done | bytes 786448 | tf_op jit(solution)/shard_map/psum | solution.py:19
  460.0 4.5 convert_reduce_fusion.1
  468.1 20.5 %all-reduce.29.cloned.1.call-done = bf16[512,768]{1,0:T(8,128)(2,1)} async-done(((bf16[512,768]{1,0:T(8,128)(2,1)}), bf16[512,768]{1,0:T(8,128)(2,1)}) %all-reduce.29.cloned.1.call-update) | async-done | bytes 786448 | tf_op jit(solution)/shard_map/psum | solution.py:19
  500.3 22.2 %while.55 = (s32[]{:T(128)}, bf16[2,256,6,64]{1,3,2,0:T(8,128)(2,1)}, bf16[2,1024,6,64]{1,3,2,0:T(8,128)(2,1)}, bf16[2,1024,6,64]{1,3,2,0:T(8,128)(2,1)}, bf16[2...) while((s32[]{:T(128)}, ...), condition=%wide.region_38.39_spmd, body=%wide.region_36.38_spmd.sunk | while | flops 1030715904 | bytes 77253888 | solution.py:88
  536.0 12.8 %copy.127 = bf16[2,1536,768]{1,0,2:T(2,128)(2,1)} copy(bf16[2,1536,768]{2,1,0:T(8,128)(2,1)} %pad_maximum_fusion.1) | data formatting | bytes 9437184 | tf_op jit(solution)/shard_map/stack | solution.py:284
  556.2 32.6 %reduce-scatter.10.cloned.1.call-done = bf16[2,256,384]{1,2,0:T(8,128)(2,1)} async-done(((bf16[2,1024,384]{1,2,0:T(8,128)(2,1)}), bf16[2,256,384]{1,2,0:T(8,128)(2,1)}) %reduce-scatter.10.cloned.1.call-update) | async-done | bytes 393232 | tf_op jit(solution)/shard_map/reduce_scatter | solution.py:227
  591.0 8.3 copy.125
  600.7 3.1 fusion.125
  616.6 308.9 %all-reduce.35.cloned.1.call-done = (bf16[2,3,768,384]{3,0,1,2:T(2,128)(2,1)}, bf16[2,384,768]{1,0,2:T(2,128)(2,1)}, bf16[2,1536,768]{1,0,2:T(2,128)(2,1)}) async-done(((bf16[2,3,768,384]{3,0,1,2:T(2,128)(2,1)}, bf16[2,384,768]{1,0,2:T(2,128)(2,1)}, bf16[2,1536,768]{1,0,2:T(2,128)(2,1)}), (bf16[2,3,768,384]{3,0,1,2:T(2,128)(2,1)}, bf16[2,384,768]{1,0,2:T(2,128)(2,1)}, ...) | async-done | bytes 9437200
  930.0 3.1 constant_dynamic-slice_fusion
  933.2 78.7 %reduce-scatter.14.cloned.1.call-done = bf16[2,192,1536]{2,1,0:T(8,128)(2,1)} async-done(((bf16[2,768,1536]{2,1,0:T(8,128)(2,1)}), bf16[2,192,1536]{2,1,0:T(8,128)(2,1)}) %reduce-scatter.14.cloned.1.call-update) | async-done | bytes 1179664 | tf_op jit(solution)/shard_map/reduce_scatter | solution.py:354
  1013.2 77.7 %all-reduce.3 = (f32[2,2,384]{2,1,0:T(2,128)}, f32[2,768]{1,0:T(2,128)}, f32[2,2,768]{2,1,0:T(2,128)}, f32[2,2,768]{2,1,0:T(2,128)}, f32[2,1536]{1,0:T(2,128)}, /*index=5*/f32[2,768]{1,0:T(2,128)}) all-reduce(f32[2,2,384]{2,1,0:T(2,128)S(1)} %pad_maximum_fusion.7, ...), channel_id=1, replica_groups=mesh['dp'=4,'seq'=4,'mp'=2] {'dp','seq'}, use_global_device_ids=true, to_apply=%region_48.49 | all-reduce | flops 13824 | bytes 110592 | tf_op jit(solution)/shard_map/psum | solution.py:367
  1093.3 42.1 %all-reduce.33.cloned.1.call-done = (bf16[2,3,192,384]{3,0,1,2:T(2,128)(2,1)}, bf16[2,384,192]{1,0,2:T(2,128)(2,1)}, bf16[2,1536,192]{1,0,2:T(2,128)(2,1)}, bf16[2,192,1536]{2,1,0:T(8,128)(2,1)}) async-done(((bf16[2,3,192,384]{3,0,1,2:T(2,128)(2,1)}, bf16[2,384,192]{1,0,2:T(2,128)(2,1)}, bf16[2,1536,192]{1,0,2:T(2,128)(2,1)}, bf16[2,192,1536]{2,1,0:T(8,128)(2,1)}), (bf16[2,3,192,384]{3,0,1,2:T(2,128)(2,1)}, ...) | async-done | bytes 3538960 | tf_op jit(solution)/shard_map/psum | solution.py:362
  (538 shorter events, 215.0 us)
Async XLA Ops:
  7.2 37.4 %all-gather.5.cloned.1.call-start = ((), (), s32[]{:S(2)}) async-start(), calls=%async_computation.5 | async-start | bytes 1966080 | tf_op jit(solution)/shard_map/all_gather | solution.py:116
  10.7 67.3 %all-gather.7.cloned.1.call-start = ((), (), s32[]{:S(2)}) async-start(), calls=%async_computation.6 | async-start | bytes 1966080 | tf_op jit(solution)/shard_map/all_gather | solution.py:115
  13.2 103.3 %all-reduce.17.cloned.1.call-start = ((), (), s32[]{:S(2)}) async-start(), calls=%async_computation.7 | async-start | bytes 1572864 | tf_op jit(solution)/shard_map/psum | solution.py:19
  97.1 58.0 %all-reduce.19.cloned.1.call-start = ((), (), s32[]{:S(2)}) async-start(), calls=%async_computation.8 | async-start | bytes 1572864 | tf_op jit(solution)/shard_map/psum | solution.py:19
  97.6 201.8 %copy-start.87 = (f32[768]{0:T(1024)}, f32[768]{0:T(1024)S(1)}, u32[]{:S(2)}) copy-start(f32[768]{0:T(1024)S(1)} %get-tuple-element.415) | copy-start | bytes 9220
  97.6 238.4 %copy-start.75 = (f32[768]{0:T(1024)}, f32[768]{0:T(1024)S(1)}, u32[]{:S(2)}) copy-start(f32[768]{0:T(1024)S(1)} %get-tuple-element.540) | copy-start | bytes 9220
  134.6 59.0 %all-gather.9.cloned.1.call-start = ((), (), s32[]{:S(2)}) async-start(), calls=%async_computation.9 | async-start | bytes 1966080 | tf_op jit(solution)/shard_map/all_gather | solution.py:116
  161.2 65.6 %all-gather.11.cloned.1.call-start = ((), (), s32[]{:S(2)}) async-start(), calls=%async_computation.10 | async-start | bytes 1966080 | tf_op jit(solution)/shard_map/all_gather | solution.py:115
  163.7 97.7 %all-reduce.21.cloned.1.call-start = ((), (), s32[]{:S(2)}) async-start(), calls=%async_computation.11 | async-start | bytes 1572864 | tf_op jit(solution)/shard_map/psum | solution.py:19
  242.0 57.3 %all-reduce.23.cloned.1.call-start = ((), (), s32[]{:S(2)}) async-start(), calls=%async_computation.12 | async-start | bytes 1572864 | tf_op jit(solution)/shard_map/psum | solution.py:19
  278.8 53.6 %all-reduce.25.cloned.1.call-start = ((), (), s32[]{:S(2)}) async-start(), calls=%async_computation.13 | async-start | bytes 1572864 | tf_op jit(solution)/shard_map/psum | solution.py:19
  311.8 82.8 %reduce-scatter.6.cloned.1.call-start = ((), (), s32[]{:S(2)}) async-start(), calls=%async_computation.14 | async-start | bytes 1966080 | tf_op jit(solution)/shard_map/reduce_scatter | solution.py:227
  362.4 66.5 %reduce-scatter.8.cloned.1.call-start = ((), (), s32[]{:S(2)}) async-start(), calls=%async_computation.15 | async-start | bytes 1966080 | tf_op jit(solution)/shard_map/reduce_scatter | solution.py:233
  363.1 90.1 %all-reduce.27.cloned.1.call-start = ((), (), s32[]{:S(2)}) async-start(), calls=%async_computation.16 | async-start | bytes 1572864 | tf_op jit(solution)/shard_map/psum | solution.py:19
  433.8 54.8 %all-reduce.29.cloned.1.call-start = ((), (), s32[]{:S(2)}) async-start(), calls=%async_computation.17 | async-start | bytes 1572864 | tf_op jit(solution)/shard_map/psum | solution.py:19
  468.1 86.7 %reduce-scatter.12.cloned.1.call-start = ((), (), s32[]{:S(2)}) async-start(), calls=%async_computation.19 | async-start | bytes 1966080 | tf_op jit(solution)/shard_map/reduce_scatter | solution.py:233
  522.5 66.3 %reduce-scatter.10.cloned.1.call-start = ((), (), s32[]{:S(2)}) async-start(), calls=%async_computation.18 | async-start | bytes 1966080 | tf_op jit(solution)/shard_map/reduce_scatter | solution.py:227
  523.1 402.4 %all-reduce.35.cloned.1.call-start = ((), (), s32[]{:S(2)}) async-start(), calls=%async_computation.23 | async-start | bytes 18874368
  599.3 412.7 %reduce-scatter.14.cloned.1.call-start = ((), (), s32[]{:S(2)}) async-start(), calls=%async_computation.21 | async-start | bytes 5898240 | tf_op jit(solution)/shard_map/reduce_scatter | solution.py:354
  608.0 482.9 %all-reduce.31.cloned.1.call-start = ((), (), s32[]{:S(2)}) async-start(), calls=%async_computation.20 | async-start | bytes 1572864 | tf_op jit(solution)/shard_map/psum | solution.py:19
  615.3 520.1 %all-reduce.33.cloned.1.call-start = ((), (), s32[]{:S(2)}) async-start(), calls=%async_computation.22 | async-start | bytes 7077888 | tf_op jit(solution)/shard_map/psum | solution.py:362
  933.1 78.9 %copy-start.104 = (f32[1536]{0:T(1024)S(1)}, f32[1536]{0:T(1024)}, u32[]{:S(2)}) copy-start(f32[1536]{0:T(1024)} %get-tuple-element.536) | copy-start | bytes 18436
  933.1 78.9 %copy-start.97 = (f32[768]{0:T(1024)S(1)}, f32[768]{0:T(1024)}, u32[]{:S(2)}) copy-start(f32[768]{0:T(1024)} %get-tuple-element.401) | copy-start | bytes 9220
  933.1 79.0 %copy-start.96 = (f32[768]{0:T(1024)S(1)}, f32[768]{0:T(1024)}, u32[]{:S(2)}) copy-start(f32[768]{0:T(1024)} %get-tuple-element.390) | copy-start | bytes 9220
  933.2 79.0 %copy-start.53 = (bf16[2,256,6,64]{1,3,2,0:T(8,128)(2,1)S(1)}, bf16[2,256,6,64]{1,3,2,0:T(8,128)(2,1)}, u32[]{:S(2)}) copy-start(bf16[2,256,6,64]{1,3,2,0:T(8,128)(2,1)} %copy-done.52) | copy-start | bytes 1179652
  933.2 79.2 %copy-start.98 = (f32[768]{0:T(1024)S(1)}, f32[768]{0:T(1024)}, u32[]{:S(2)}) copy-start(f32[768]{0:T(1024)} %get-tuple-element.509) | copy-start | bytes 9220
  933.2 79.2 %copy-start.95 = (f32[768]{0:T(1024)S(1)}, f32[768]{0:T(1024)}, u32[]{:S(2)}) copy-start(f32[768]{0:T(1024)} %get-tuple-element.403) | copy-start | bytes 9220
  933.2 79.2 %copy-start.62 = (bf16[2,256,384]{1,2,0:T(8,128)(2,1)S(1)}, bf16[2,256,384]{1,2,0:T(8,128)(2,1)}, u32[]{:S(2)}) copy-start(bf16[2,256,384]{1,2,0:T(8,128)(2,1)} %reduce-scatter.8.cloned.1.call-done) | copy-start | bytes 1179652
  933.2 79.4 %copy-start.105 = (f32[1536]{0:T(1024)S(1)}, f32[1536]{0:T(1024)}, u32[]{:S(2)}) copy-start(f32[1536]{0:T(1024)} %get-tuple-element.538) | copy-start | bytes 18436
  933.2 79.4 %copy-start.92 = (f32[768]{0:T(1024)S(1)}, f32[768]{0:T(1024)}, u32[]{:S(2)}) copy-start(f32[768]{0:T(1024)} %get-tuple-element.400) | copy-start | bytes 9220
  933.2 79.5 %copy-start.91 = (f32[768]{0:T(1024)S(1)}, f32[768]{0:T(1024)}, u32[]{:S(2)}) copy-start(f32[768]{0:T(1024)} %get-tuple-element.392) | copy-start | bytes 9220
  933.2 79.5 %copy-start.51 = (bf16[2,256,6,64]{1,3,2,0:T(8,128)(2,1)S(1)}, bf16[2,256,6,64]{1,3,2,0:T(8,128)(2,1)}, u32[]{:S(2)}) copy-start(bf16[2,256,6,64]{1,3,2,0:T(8,128)(2,1)} %get-tuple-element.203) | copy-start | bytes 1179652
  (125 other events, 1208.7 us)
Sparse Core Ops, SparseCore 0:
  10.8 33.6 all-gather.4
  47.0 30.9 all-gather.6
  97.2 19.1 all-reduce.16
  134.7 20.3 all-reduce.18
  161.3 32.1 all-gather.8
  195.8 30.9 all-gather.10
  242.2 19.1 all-reduce.20
  278.9 20.3 all-reduce.22
  311.9 20.4 all-reduce.24
  362.5 32.1 reduce-scatter.5
  397.9 30.9 reduce-scatter.7
  434.0 19.1 all-reduce.26
  468.2 20.3 all-reduce.28
  522.6 32.1 reduce-scatter.11
  557.9 30.9 reduce-scatter.9
  599.4 326.0 all-reduce.34
  927.7 84.1 reduce-scatter.13
  1014.9 19.7 all-reduce.30
  1039.2 96.1 all-reduce.32
where the time goes:
time: 1160 us; the launch traced here: 1150 us
  waiting for transfers between devices  777 us (67%)
  matrix products  134 us (12%)
  local copies, waits for them, and re-layouts  82.9 us (7%)
  blocking collectives  77.7 us (7%)
  other arithmetic  57.8 us (5%)
  between operations  16.5 us (1%)
    unnamed x20, waiting for transfers between devices  310 us
    psum x8, waiting for transfers between devices, head_total(): return lax.psum(partial_sum.astype(jnp.bfloat16), 'mp').astype(jnp.float32)  136 us
    reduce_scatter x1, waiting for transfers between devices, local(): lax.psum_scatter(up_part.astype(jnp.bfloat16), 'dp', scatter_dimension=1,...  78.7 us
    psum x1, blocking collectives, local(): lax.psum((qv_part, out_bias_part, gain_part, shift_part, up_bias_part, do...  77.7 us
    all_gather x2, waiting for transfers between devices, layer_forward(): lax.all_gather(keys, 'seq', axis=1, tiled=True)  61.5 us
    reduce_scatter x2, waiting for transfers between devices, layer_backward(): lax.psum_scatter(grad_key.reshape(batch, full, local_width).astype(jnp.bf...  60.8 us
    all_gather x2, waiting for transfers between devices, layer_forward(): lax.all_gather(values, 'seq', axis=1, tiled=True)  56.5 us
    dot_general x12, matrix products, dot_float(): return jnp.dot(left, right, preferred_element_type=jnp.float32)  45.4 us
  transfers between devices with their start and end apart: 19, of which 18 were waited for; matrix products, arithmetic and copies ran while one was open for 7% of the time, Pallas kernels for 0%

commit v1 on v0

v1 whole, which is shorter than its diff:
```python
import jax
import jax.numpy as jnp
from jax import lax
from jax.sharding import PartitionSpec as P

HEAD = 64
eps_norm = 1e-05
root_half = 0.7071067811865476
inv_root_tau = 0.3989422804014327
f32 = jnp.float32
bf16 = jnp.bfloat16


def dot_nn(left, right):
    return lax.dot_general(left, right, (((1,), (0,)), ((), ())), preferred_element_type=f32)


def dot_nt(left, right):
    return lax.dot_general(left, right, (((1,), (1,)), ((), ())), preferred_element_type=f32)


def dot_tn(left, right):
    return lax.dot_general(left, right, (((0,), (0,)), ((), ())), preferred_element_type=f32)


def swap(value, axis, mask):
    count = lax.axis_size(axis)
    return lax.ppermute(value, axis, [(i, i ^ mask) for i in range(count)])


def place_bit(axis, bit):
    return (lax.axis_index(axis) >> bit) & 1


def bits_of(axis):
    count = lax.axis_size(axis)
    number = count.bit_length() - 1
    assert 1 << number == count
    return number


def pick(value, index, axis):
    return lax.dynamic_index_in_dim(value, index, axis, keepdims=False)


def mp_sum(partial_sum):
    own = partial_sum.astype(bf16)
    return own.astype(f32) + swap(own, "mp", 1).astype(f32)


def add_low(left, right):
    return (left.astype(f32) + right.astype(f32)).astype(bf16)


def normalize(rows_in, gain, shift):
    center = rows_in - jnp.mean(rows_in, axis=-1, keepdims=True)
    scale = lax.rsqrt(jnp.mean(center * center, axis=-1, keepdims=True) + eps_norm)
    unit = center * scale
    return (unit * gain + shift, unit, scale)


def normalize_back(grad_out, unit, scale, gain):
    grad_unit = grad_out * gain
    inner = (
        grad_unit
        - jnp.mean(grad_unit, axis=-1, keepdims=True)
        - unit * jnp.mean(grad_unit * unit, axis=-1, keepdims=True)
    )
    return (inner * scale, jnp.sum(grad_out * unit, axis=0), jnp.sum(grad_out, axis=0))


def share_halves(half):
    other = swap(half, "mp", 1)
    first = lax.axis_index("mp") == 0
    return jnp.where(first, jnp.stack([half, other]), jnp.stack([other, half])).reshape(
        (2 * half.shape[0],) + half.shape[1:]
    )


def from_far(value, mask):
    count = value.shape[0] // 2
    mine = pick(value.reshape((2, count) + value.shape[1:]), lax.axis_index("mp"), 0)
    return share_halves(swap(mine, "seq", mask))


def reduce_bundle(grad, order):
    shares = lax.axis_size("dp")
    width = grad.shape[0] // shares
    keep = grad.reshape(shares, width, grad.shape[1])
    arrived = None
    steps = [("seq", order[0])] + [("dp", b) for b in range(bits_of("dp"))]
    steps += [("seq", b) for b in order[1:]]

    def part(value, axis, bit, side):
        if axis == "seq":
            half = value.shape[2] // 2
            return lax.dynamic_slice_in_dim(value, side * half, half, 2)
        shaped = value.reshape(value.shape[0] // 2, 2, width, value.shape[2])
        return pick(shaped, side, 1)

    for axis, bit in steps:
        mine = place_bit(axis, bit)
        send = part(keep, axis, bit, 1 - mine)
        keep_next = part(keep, axis, bit, mine)
        if arrived is not None:
            send = add_low(send, part(arrived, axis, bit, 1 - mine))
            keep_next = add_low(keep_next, part(arrived, axis, bit, mine))
        arrived = swap(send.astype(bf16), axis, 1 << bit)
        keep = keep_next
    total = add_low(keep, arrived)[0]
    for bit in reversed(order):
        other = swap(total, "seq", 1 << bit)
        first = place_bit("seq", bit) == 0
        total = jnp.where(
            first,
            jnp.concatenate([total, other], axis=1),
            jnp.concatenate([other, total], axis=1),
        )
    return total


def split_heads(value):
    return value.reshape(value.shape[0], value.shape[1] // HEAD, HEAD)


def attend(query, key_all, value_all, same):
    scores = (
        jnp.einsum("qhd,khd->hqk", split_heads(query), split_heads(key_all), preferred_element_type=f32)
        * 0.125
    )
    scores = jnp.where(same[None], scores, -1e30)
    peak = jnp.max(scores, axis=-1, keepdims=True)
    raised = jnp.exp(scores - peak)
    total = jnp.sum(raised, axis=-1, keepdims=True)
    weights = (raised / total).astype(bf16)
    context = jnp.einsum("hqk,khd->qhd", weights, split_heads(value_all), preferred_element_type=f32)
    return (context.astype(bf16).reshape(query.shape), peak[..., 0] + jnp.log(total[..., 0]))


def attend_back(query, key_all, value_all, same, log_total, grad_context):
    query, key_all, value_all, grad_context = map(
        split_heads, (query, key_all, value_all, grad_context)
    )
    scores = jnp.einsum("qhd,khd->hqk", query, key_all, preferred_element_type=f32) * 0.125
    chance = jnp.where(same[None], jnp.exp(scores - log_total[..., None]), 0.0)
    grad_chance = jnp.einsum("qhd,khd->hqk", grad_context, value_all, preferred_element_type=f32)
    grad_value = jnp.einsum("hqk,qhd->khd", chance.astype(bf16), grad_context, preferred_element_type=f32)
    grad_score = chance * (grad_chance - jnp.sum(grad_chance * chance, axis=-1, keepdims=True))
    grad_score = grad_score.astype(bf16)
    grad_query = jnp.einsum("hqk,khd->qhd", grad_score, key_all, preferred_element_type=f32) * 0.125
    grad_key = jnp.einsum("hqk,qhd->khd", grad_score, query, preferred_element_type=f32) * 0.125

    def joined(value):
        return value.astype(bf16).reshape(value.shape[0], -1)

    return joined(grad_query), joined(grad_key), joined(grad_value)


def layer_forward(inputs, low_own, low_others, same, params):
    (
        weight_qkv,
        bias_qv,
        weight_out,
        bias_out,
        gain,
        shift,
        weight_up,
        bias_up,
        weight_down,
        bias_down,
    ) = params
    low_all = jnp.concatenate([low_own] + low_others, axis=0)
    query = (dot_nn(low_own, weight_qkv[0]) + bias_qv[0]).astype(bf16)
    keys = dot_nn(low_all, weight_qkv[1]).astype(bf16)
    values = (dot_nn(low_all, weight_qkv[2]) + bias_qv[1]).astype(bf16)
    context, log_total = attend(query, keys, values, same)
    attended = mp_sum(dot_nn(context, weight_out)) + bias_out
    hidden, unit_one, scale_one = normalize(inputs + attended, gain[0], shift[0])
    low_hidden = hidden.astype(bf16)
    pre_act = dot_nn(low_hidden, weight_up) + bias_up
    low_act = jax.nn.gelu(pre_act, approximate=False).astype(bf16)
    mixed = mp_sum(dot_nn(low_act, weight_down)) + bias_down
    result, unit_two, scale_two = normalize(hidden + mixed, gain[1], shift[1])
    saved = (
        low_all,
        query,
        keys,
        values,
        log_total,
        context,
        unit_one,
        scale_one,
        low_hidden,
        pre_act,
        low_act,
        unit_two,
        scale_two,
    )
    return (result, saved)


def layer_backward(grad_flat, saved, same, params, orders):
    (
        weight_qkv,
        bias_qv,
        weight_out,
        bias_out,
        gain,
        shift,
        weight_up,
        bias_up,
        weight_down,
        bias_down,
    ) = params
    (
        low_all,
        query,
        keys,
        values,
        log_total,
        context,
        unit_one,
        scale_one,
        low_hidden,
        pre_act,
        low_act,
        unit_two,
        scale_two,
    ) = saved
    span = grad_flat.shape[0]
    grad_mixed, gain_two, shift_two = normalize_back(grad_flat, unit_two, scale_two, gain[1])
    grad_bias_down = jnp.sum(grad_mixed, axis=0)
    low_mixed = grad_mixed.astype(bf16)
    down_sum = reduce_bundle(dot_tn(low_mixed, low_act).astype(bf16), orders[0])
    grad_act = dot_nt(low_mixed, weight_down)
    normal_cdf = 0.5 * (1.0 + lax.erf(pre_act * root_half))
    density = jnp.exp(-0.5 * pre_act * pre_act) * inv_root_tau
    low_pre = (grad_act * (normal_cdf + pre_act * density)).astype(bf16)
    grad_bias_up = jnp.sum(low_pre.astype(f32), axis=0)
    up_sum = reduce_bundle(dot_tn(low_hidden, low_pre).astype(bf16), orders[1])
    grad_hidden = grad_mixed + mp_sum(dot_nt(low_pre, weight_up))
    grad_attended, gain_one, shift_one = normalize_back(grad_hidden, unit_one, scale_one, gain[0])
    grad_bias_out = jnp.sum(grad_attended, axis=0)
    low_attended = grad_attended.astype(bf16)
    grad_context = dot_nt(low_attended, weight_out).astype(bf16)
    grad_query, grad_key, grad_value = attend_back(query, keys, values, same, log_total, grad_context)

    low_own = low_all[:span]
    attn_sum = reduce_bundle(
        jnp.concatenate(
            [
                dot_tn(low_own, grad_query).astype(bf16),
                dot_tn(low_all, grad_key).astype(bf16),
                dot_tn(low_all, grad_value).astype(bf16),
                dot_tn(low_attended, context).astype(bf16),
            ],
            axis=1,
        ),
        orders[2],
    )
    place = lax.axis_index("mp")
    back_kv = dot_nt(grad_key, weight_qkv[1]) + dot_nt(grad_value, weight_qkv[2])
    parts = back_kv.shape[0] // span
    back_kv = back_kv.reshape(parts, 2, span // 2, back_kv.shape[1])
    back_own = back_kv[0] + dot_nt(grad_query, weight_qkv[0]).reshape(back_kv.shape[1:])

    def half_sum(value):
        send = pick(value, 1 - place, 0).astype(bf16)
        return pick(value, place, 0).astype(bf16).astype(f32) + swap(send, "mp", 1).astype(f32)

    total_half = half_sum(back_own)
    for j in range(1, parts):
        total_half = total_half + swap(half_sum(back_kv[j]).astype(bf16), "seq", 2 * j).astype(f32)
    back_total = share_halves(total_half.astype(bf16))
    grad_inputs = grad_attended + back_total.astype(f32)
    small = (
        jnp.stack(
            [jnp.sum(grad_query.astype(f32), axis=0), jnp.sum(grad_value.astype(f32), axis=0)]
        ),
        grad_bias_out,
        jnp.stack([gain_one, gain_two]),
        jnp.stack([shift_one, shift_two]),
        grad_bias_up,
        grad_bias_down,
    )
    return (grad_inputs, small, (attn_sum, up_sum, down_sum))


def layer_part(index, params):
    return tuple((array[index] for array in params))


def stack_pair(first_part, second_part):
    return jnp.stack([first_part, second_part])


def local(
    tokens,
    segments,
    dropped,
    qkv_weight,
    qv_bias,
    out_weight,
    out_bias,
    norm_gain,
    norm_shift,
    up_weight,
    up_bias,
    down_weight,
    down_bias,
    cotangent,
):
    params = (
        qkv_weight,
        qv_bias,
        out_weight,
        out_bias,
        norm_gain,
        norm_shift,
        up_weight,
        up_bias,
        down_weight,
        down_bias,
    )
    first = layer_part(0, params)
    second = layer_part(1, params)
    rows_here, span, width = tokens.shape
    assert rows_here == 2
    places = lax.axis_size("seq")
    place = lax.axis_index("seq")
    row = place & 1
    tokens_mine = pick(tokens, row, 0)
    tokens_partner = pick(tokens, 1 - row, 0)
    chunks = [tokens_mine]
    for c in range(1, places):
        chunks.append(from_far(tokens_mine if c % 2 == 0 else tokens_partner, c))
    low_own = jnp.concatenate(chunks[:2], axis=0)
    low_others = [jnp.concatenate(chunks[c : c + 2], axis=0) for c in range(2, places, 2)]
    seg_row = pick(segments, row, 0).reshape(places, span)
    for bit in range(bits_of("seq")):
        shaped = seg_row.reshape(places >> (bit + 1), 2, 1 << bit, span)
        seg_row = jnp.where(place_bit("seq", bit) == 1, shaped[:, ::-1], shaped).reshape(places, span)
    seg_keys = seg_row.reshape(places * span)
    same = seg_keys[: 2 * span, None] == seg_keys[None, :]
    cot_mine = pick(cotangent, row, 0)
    cot_far = from_far(pick(cotangent, 1 - row, 0), 1)
    cot_float = jnp.concatenate([cot_mine, cot_far], axis=0).astype(f32)
    kept = lax.dynamic_index_in_dim(dropped, lax.axis_index("dp") * rows_here + row, 0, keepdims=False) == 0

    hidden_one, saved_one = layer_forward(low_own.astype(f32), low_own, low_others, same, first)
    low_one = hidden_one.astype(bf16)
    others_one = [from_far(low_one, c) for c in range(2, places, 2)]
    result_two, saved_two = layer_forward(hidden_one, low_one, others_one, same, second)
    result = jnp.where(kept, result_two, hidden_one)

    def send_back(value):
        mine, partner = value[:span], value[span:].astype(bf16)
        arrived = from_far(partner, 1).astype(f32)
        return jnp.where(row == 0, jnp.stack([mine, arrived]), jnp.stack([arrived, mine]))

    outputs = send_back(result)
    grad_two = jnp.where(kept, cot_float, 0.0)
    up_down = list(range(bits_of("seq")))
    down_up = up_down[::-1]
    grad_in_two, small_two, big_two = layer_backward(
        grad_two, saved_two, same, second, (up_down, down_up, up_down)
    )
    grad_hidden_one = jnp.where(kept, grad_in_two, cot_float)
    grad_tokens, small_one, big_one = layer_backward(
        grad_hidden_one, saved_one, same, first, (down_up, up_down, down_up)
    )
    tokens_grad = send_back(grad_tokens)
    small = jax.tree.map(stack_pair, small_one, small_two)
    qv_sum, out_bias_sum, gain_sum, shift_sum, up_bias_sum, down_bias_sum = lax.psum(small, ("dp", "seq"))

    def attn_parts(total):
        quarter = total.shape[1] // 4
        pieces = [total[:, i * quarter : (i + 1) * quarter].astype(f32) for i in range(4)]
        return jnp.stack(pieces[:3]), pieces[3].T

    qkv_sum, out_sum = jax.tree.map(stack_pair, attn_parts(big_one[0]), attn_parts(big_two[0]))
    up_sum = jnp.stack([big_one[1].astype(f32), big_two[1].astype(f32)])
    down_sum = jnp.stack([big_one[2].astype(f32).T, big_two[2].astype(f32).T])
    return (
        outputs,
        tokens_grad,
        qkv_sum,
        qv_sum,
        out_sum,
        out_bias_sum,
        gain_sum,
        shift_sum,
        up_sum,
        up_bias_sum,
        down_sum,
        down_bias_sum,
    )


def solution(mesh):
    placed = (
        P("dp", "seq", None),
        P("dp", None),
        P(),
        P(None, None, None, "mp"),
        P(None, None, "mp"),
        P(None, "mp", None),
        P(),
        P(),
        P(),
        P(None, None, "mp"),
        P(None, "mp"),
        P(None, "mp", None),
        P(),
        P("dp", "seq", None),
    )
    return jax.shard_map(
        local,
        mesh=mesh,
        in_specs=placed,
        out_specs=(
            P("dp", "seq", None),
            P("dp", "seq", None),
            P(None, None, "dp", "mp"),
            P(None, None, "mp"),
            P(None, "mp", "dp"),
            P(),
            P(),
            P(),
            P(None, "dp", "mp"),
            P(None, "mp"),
            P(None, "mp", "dp"),
            P(),
        ),
        check_vma=False,
    )
```

time: 1160 us -> 536 us (0.46)
  waiting for transfers between devices: 777 us -> 171 us
  starting transfers between devices: 2.68 us -> 50.6 us
  local copies, waits for them, and re-layouts: 82.9 us -> 43.5 us
  between operations: 16.5 us -> 3.81 us
  other arithmetic: 57.8 us -> 69.4 us
    unnamed x20 -> x0, waiting for transfers between devices: 310 us -> none
    psum x9 -> x0, waiting for transfers between devices: 178 us -> none  [the longest x8 136 us: head_total(): return lax.psum(partial_sum.astype(jnp.bfloat16), 'mp').astype(jnp.float32)]
    ppermute x0 -> x64, waiting for transfers between devices: none -> 171 us  [swap(): return lax.ppermute(value, axis, [(i, i ^ mask) for i in range(count)])]
    reduce_scatter x5 -> x0, waiting for transfers between devices: 170 us -> none  [the longest x1 78.7 us: local(): lax.psum_scatter(up_part.astype(jnp.bfloat16), 'dp', scatter_dimension=1,...]
    all_gather x4 -> x0, waiting for transfers between devices: 118 us -> none  [the longest x2 61.5 us: layer_forward(): lax.all_gather(keys, 'seq', axis=1, tiled=True)]
    ppermute x0 -> x64, starting transfers between devices: none -> 50.6 us  [swap(): return lax.ppermute(value, axis, [(i, i ^ mask) for i in range(count)])]
    another operation x9 -> x8, local copies, waits for them, and re-layouts: 24 us -> 0.15 us  [stack_pair(): return jnp.stack([first_part, second_part])]
    unnamed x249 -> x221, local copies, waits for them, and re-layouts: 29.1 us -> 8.96 us
  transfers between devices with their start and end apart: 19 -> 64, of which waited for: 18 -> 33; matrix products, arithmetic and copies ran while one was open for 7% -> 32% of each run, Pallas kernels for 0% -> 0%
where the time goes in v1:
time: 536 us; the launch traced here: 535 us
  waiting for transfers between devices  171 us (32%)
  matrix products  123 us (23%)
  blocking collectives  72.8 us (14%)
  other arithmetic  69.4 us (13%)
  starting transfers between devices  50.6 us (9%)
  local copies, waits for them, and re-layouts  43.5 us (8%)
    ppermute x64, waiting for transfers between devices, swap(): return lax.ppermute(value, axis, [(i, i ^ mask) for i in range(count)])  171 us
    psum x1, blocking collectives, local(): lax.psum(small, ('dp', 'seq'))  72.8 us
    ppermute x64, starting transfers between devices, swap(): return lax.ppermute(value, axis, [(i, i ^ mask) for i in range(count)])  50.6 us
    dot_general x12, matrix products, dot_nn(): lax.dot_general(left, right, (((1,), (0,)), ((), ())), preferred_element_...  42.3 us
    dot_general x12, matrix products, dot_nt(): lax.dot_general(left, right, (((1,), (1,)), ((), ())), preferred_element_...  24.2 us
    dot_general x2, matrix products, attend_back(): jnp.einsum('qhd,khd->hqk', grad_context, value_all, preferred_element_typ...  15.4 us
    dot_general x12, matrix products, dot_tn(): lax.dot_general(left, right, (((0,), (0,)), ((), ())), preferred_element_...  14.8 us
    convert_element_type x2, other arithmetic, attend_back(): grad_score = grad_score.astype(bf16)  14.1 us
  transfers between devices with their start and end apart: 64, of which 33 were waited for; matrix products, arithmetic and copies ran while one was open for 32% of the time, Pallas kernels for 0%

profile of v1, /device:TPU:0, one launch (start us, length us, event | category | flops | bytes accessed | tf_op | source)
XLA Modules:
  0.0 534.6 jit_solution(1466307572794170447)
XLA Ops:
  1.9 4.0 collective-permute-start.4
  6.8 8.2 %collective-permute-done.2 = bf16[128,768]{1,0:T(8,128)(2,1)S(1)} collective-permute-done((bf16[128,768]{1,0:T(8,128)(2,1)S(1)}, bf16[128,768]{1,0:T(8,128)(2,1)S(1)}, u32[]{:S(2)}, u32[]{:S(2)}) %collective-permute-start.2) | collective-permute-done | bytes 196640 | tf_op jit(solution)/shard_map/ppermute | solution.py:28
  24.0 3.6 fusion
  29.6 4.3 fusion.97
  37.8 9.5 %fusion.14 = (bf16[512,1536]{1,0:T(8,128)(2,1)S(1)}, f32[512,1536]{1,0:T(8,128)}) fusion(f32[1536]{0:T(1024)S(1)} %get-tuple-element.36, bf16[2,768,1536]{2,1,0:T(8,128)(2,1)S(1)} %bitcast.514, f32[512,768]{1,0:T(8,128)S(1)} %get-tuple-element.70, f32[768]{0:T(1024)S(1)} %get-tuple-element.34, f32[768]{0:T(1024)S(1)} %get-tuple-element.145, ...), kind=kOutput, calls=%fused_computation.36 | convolution fusion | flops 1261830144 | bytes 8671232 | tf_op jit(solution)/shard_map/dot_general | solution.py:15
  54.3 9.5 %collective-permute-done.8 = bf16[256,768]{1,0:T(8,128)(2,1)S(1)} collective-permute-done((bf16[256,768]{1,0:T(8,128)(2,1)S(1)}, bf16[256,768]{1,0:T(8,128)(2,1)S(1)}, u32[]{:S(2)}, u32[]{:S(2)}) %collective-permute-start.8) | collective-permute-done | bytes 393248 | tf_op jit(solution)/shard_map/ppermute | solution.py:28
  63.8 13.3 %fusion.93 = bf16[512,384]{0,1:T(8,128)(2,1)S(1)} fusion(bf16[512,768]{1,0:T(8,128)(2,1)S(1)} %fusion.98, bf16[2,3,768,384]{3,2,1,0:T(8,128)(2,1)S(1)} %copy-done.18, f32[384]{0:T(512)S(1)} %get-tuple-element.42), kind=kOutput, calls=%fused_computation.187 | convolution fusion | flops 302383104 | bytes 1771520 | tf_op jit(solution)/shard_map/dot_general | solution.py:15
  81.4 3.6 fusion.1
  85.9 4.0 fusion.96
  94.1 9.6 %fusion.17 = (bf16[512,1536]{1,0:T(8,128)(2,1)S(1)}, f32[512,1536]{1,0:T(8,128)}) fusion(f32[1536]{0:T(1024)S(1)} %get-tuple-element.37, bf16[2,768,1536]{2,1,0:T(8,128)(2,1)S(1)} %bitcast.514, f32[512,768]{1,0:T(8,128)S(1)} %get-tuple-element.66, f32[768]{0:T(1024)S(1)} %get-tuple-element.35, f32[768]{0:T(1024)S(1)} %get-tuple-element.144, ...), kind=kOutput, calls=%fused_computation.39 | convolution fusion | flops 1261830144 | bytes 8671232 | tf_op jit(solution)/shard_map/dot_general | solution.py:15
  115.5 4.1 convert_reduce_fusion
  138.0 7.7 %multiply_reduce_fusion.1 = (f32[6,512]{1,0:T(8,128)S(1)}, f32[6,512,1024]{2,1,0:T(8,128)}) fusion(f32[6,512,1024]{2,1,0:T(8,128)S(1)} %bitcast.397, f32[6,512]{1,0:T(8,128)S(1)} %log_add_fusion.1, pred[512,1024]{1,0:T(8,128)(4,1)S(1)} %broadcast_compare_fusion, bf16[512,6,64]{0,2,1:T(8,128)(2,1)S(1)} %bitcast.456, bf16[1024,6,64]{0,2,1:T(8,128)(2,1)S(1)} %bitcast.468), kind=kOutput, calls=%fused_computation.4 | convolution fusion | flops 418378752 | bytes 26894336 | tf_op jit(solution)/shard_map/qhd,khd->hqk/dot_general | solution.py:146
  145.7 7.0 %multiply_convert_fusion.1 = bf16[6,512,1024]{2,1,0:T(8,128)(2,1)S(1)} fusion(f32[6,512,1024]{2,1,0:T(8,128)} %get-tuple-element.129, f32[6,512,1024]{2,1,0:T(8,128)S(1)} %bitcast.397, f32[6,512]{1,0:T(8,128)S(1)} %get-tuple-element.128, f32[6,512]{1,0:T(8,128)S(1)} %log_add_fusion.1, pred[512,1024]{1,0:T(8,128)(4,1)S(1)} %broadcast_compare_fusion), kind=kLoop, calls=%fused_computation.3 | loop fusion | flops 18874368 | bytes 32006144 | tf_op jit(solution)/shard_map/convert_element_type | solution.py:149
  165.2 4.3 copy.35
  184.6 5.0 collective-permute-done.19
  190.9 6.1 %collective-permute-done.59 = bf16[2,192,768]{2,1,0:T(8,128)(2,1)S(1)} collective-permute-done((bf16[2,192,768]{2,1,0:T(8,128)(2,1)S(1)}, bf16[2,192,768]{2,1,0:T(8,128)(2,1)S(1)}, u32[]{:S(2)}, u32[]{:S(2)}) %collective-permute-start.59) | collective-permute-done | bytes 589856 | tf_op jit(solution)/shard_map/ppermute | solution.py:28
  200.0 14.7 %collective-permute-done.47 = bf16[2,192,768]{2,1,0:T(8,128)(2,1)S(1)} collective-permute-done((bf16[2,192,768]{2,1,0:T(8,128)(2,1)S(1)}, bf16[2,192,768]{2,1,0:T(8,128)(2,1)S(1)}, u32[]{:S(2)}, u32[]{:S(2)}) %collective-permute-start.47) | collective-permute-done | bytes 589856 | tf_op jit(solution)/shard_map/ppermute | solution.py:28
  255.7 23.9 %collective-permute-done.51 = bf16[192,768]{1,0:T(8,128)(2,1)S(1)} collective-permute-done((bf16[192,768]{1,0:T(8,128)(2,1)S(1)}, bf16[192,768]{1,0:T(8,128)(2,1)S(1)}, u32[]{:S(2)}, u32[]{:S(2)}) %collective-permute-start.51) | collective-permute-done | bytes 294944 | tf_op jit(solution)/shard_map/ppermute | solution.py:28
  291.6 7.7 %multiply_reduce_fusion = (f32[6,512]{1,0:T(8,128)S(1)}, f32[6,512,1024]{2,1,0:T(8,128)}) fusion(f32[6,512,1024]{2,1,0:T(8,128)S(1)} %bitcast.395, f32[6,512]{1,0:T(8,128)S(1)} %log_add_fusion, pred[512,1024]{1,0:T(8,128)(4,1)S(1)} %broadcast_compare_fusion, bf16[512,6,64]{0,2,1:T(8,128)(2,1)S(1)} %bitcast.458, bf16[1024,6,64]{0,2,1:T(8,128)(2,1)S(1)} %bitcast.466), kind=kOutput, calls=%fused_computation.1 | convolution fusion | flops 418378752 | bytes 26894336 | tf_op jit(solution)/shard_map/qhd,khd->hqk/dot_general | solution.py:146
  299.3 7.0 %multiply_convert_fusion = bf16[6,512,1024]{2,1,0:T(8,128)(2,1)S(1)} fusion(f32[6,512,1024]{2,1,0:T(8,128)} %get-tuple-element.131, f32[6,512,1024]{2,1,0:T(8,128)S(1)} %bitcast.395, f32[6,512]{1,0:T(8,128)S(1)} %get-tuple-element.130, f32[6,512]{1,0:T(8,128)S(1)} %log_add_fusion, pred[512,1024]{1,0:T(8,128)(4,1)S(1)} %broadcast_compare_fusion), kind=kLoop, calls=%fused_computation | loop fusion | flops 18874368 | bytes 32006144 | tf_op jit(solution)/shard_map/convert_element_type | solution.py:149
  323.6 4.3 copy.34
  342.3 20.7 %collective-permute-done.37 = bf16[1,192,384]{2,1,0:T(8,128)(2,1)S(1)} collective-permute-done((bf16[1,192,384]{2,1,0:T(8,128)(2,1)S(1)}, bf16[1,192,384]{2,1,0:T(8,128)(2,1)S(1)}, u32[]{:S(2)}, u32[]{:S(2)}) %collective-permute-start.37) | collective-permute-done | bytes 147488 | tf_op jit(solution)/shard_map/ppermute | solution.py:28
  365.8 72.8 %all-reduce = (f32[2,2,384]{2,1,0:T(2,128)}, f32[2,768]{1,0:T(2,128)}, f32[2,2,768]{2,1,0:T(2,128)}, f32[2,2,768]{2,1,0:T(2,128)}, f32[2,1536]{1,0:T(2,128)}, /*index=5*/f32[2,768]{1,0:T(2,128)}) all-reduce(f32[2,2,384]{2,1,0:T(2,128)S(1)} %pad_maximum_fusion.11, ...), channel_id=1, replica_groups=mesh['dp'=4,'seq'=4,'mp'=2] {'dp','seq'}, use_global_device_ids=true, to_apply=%region_26.27 | all-reduce | flops 13824 | bytes 110592 | tf_op jit(solution)/shard_map/psum | solution.py:374
  448.4 10.5 %collective-permute-done.24 = bf16[256,768]{1,0:T(8,128)(2,1)S(1)} collective-permute-done((bf16[256,768]{1,0:T(8,128)(2,1)S(1)}, bf16[256,768]{1,0:T(8,128)(2,1)S(1)}, u32[]{:S(2)}, u32[]{:S(2)}) %collective-permute-start.24) | collective-permute-done | bytes 393248 | tf_op jit(solution)/shard_map/ppermute | solution.py:28
  459.5 10.1 %collective-permute-done.41 = bf16[2,192,768]{2,1,0:T(8,128)(2,1)S(1)} collective-permute-done((bf16[2,192,768]{2,1,0:T(8,128)(2,1)S(1)}, bf16[2,192,768]{2,1,0:T(8,128)(2,1)S(1)}, u32[]{:S(2)}, u32[]{:S(2)}) %collective-permute-start.41) | collective-permute-done | bytes 589856 | tf_op jit(solution)/shard_map/ppermute | solution.py:28
  474.8 8.0 %collective-permute-done.54 = bf16[1,192,768]{2,1,0:T(8,128)(2,1)S(1)} collective-permute-done((bf16[1,192,768]{2,1,0:T(8,128)(2,1)S(1)}, bf16[1,192,768]{2,1,0:T(8,128)(2,1)S(1)}, u32[]{:S(2)}, u32[]{:S(2)}) %collective-permute-start.54) | collective-permute-done | bytes 294944 | tf_op jit(solution)/shard_map/ppermute | solution.py:28
  485.0 3.9 collective-permute-done.42
  490.0 4.6 collective-permute-done.43
  497.0 4.3 collective-permute-done.44
  506.3 8.2 %collective-permute-done.30 = bf16[1,192,768]{2,1,0:T(8,128)(2,1)S(1)} collective-permute-done((bf16[1,192,768]{2,1,0:T(8,128)(2,1)S(1)}, bf16[1,192,768]{2,1,0:T(8,128)(2,1)S(1)}, u32[]{:S(2)}, u32[]{:S(2)}) %collective-permute-start.30) | collective-permute-done | bytes 294944 | tf_op jit(solution)/shard_map/ppermute | solution.py:28
  520.6 4.4 collective-permute-done.32
  527.2 4.8 collective-permute-done.33
  (550 shorter events, 217.2 us)
Async XLA Ops:
  1.9 13.5 %collective-permute-start.4 = (bf16[128,768]{1,0:T(8,128)(2,1)S(1)}, bf16[128,768]{1,0:T(8,128)(2,1)S(1)}, u32[]{:S(2)}, u32[]{:S(2)}) collective-permute-start(bf16[128,768]{1,0:T(8,128)(2,1)S(1)} %dynamic-slice_bitcast_fusion.6), channel_id=1, source_target_pairs={{0,6},{2,4},{4,2},{6,0},{1,7},{3,5},{5,3},{7,1},{8,14},{10,12},{12... | collective-permute-start | bytes 589832 | tf_op jit(solution)/shard_map/ppermute | solution.py:28
  63.8 13.3 %collective-permute-start.9 = (bf16[256,768]{1,0:T(8,128)(2,1)S(1)}, bf16[256,768]{1,0:T(8,128)(2,1)S(1)}, u32[]{:S(2)}, u32[]{:S(2)}) collective-permute-start(bf16[256,768]{1,0:T(8,128)(2,1)S(1)} %collective-permute-done.8), channel_id=1, source_target_pairs={{0,1},{1,0},{2,3},{3,2},{4,5},{5,4},{6,7},{7,6},{8,9},{9,8},{10,11... | collective-permute-start | bytes 1179656 | tf_op jit(solution)/shard_map/ppermute | solution.py:28
  91.2 15.1 %collective-permute-start.14 = (bf16[128,768]{1,0:T(8,128)(2,1)S(1)}, bf16[128,768]{1,0:T(8,128)(2,1)S(1)}, u32[]{:S(2)}, u32[]{:S(2)}) collective-permute-start(bf16[128,768]{1,0:T(8,128)(2,1)S(1)} %dynamic-slice_bitcast_fusion.3), channel_id=1, source_target_pairs={{0,2},{2,0},{4,6},{6,4},{1,3},{3,1},{5,7},{7,5},{8,10},{10,8},{12,... | collective-permute-start | bytes 589832 | tf_op jit(solution)/shard_map/ppermute | solution.py:28
  124.7 54.0 %collective-permute-start.58 = (bf16[4,192,768]{2,1,0:T(8,128)(2,1)}, bf16[4,192,768]{2,1,0:T(8,128)(2,1)}, u32[]{:S(2)}, u32[]{:S(2)}) collective-permute-start(bf16[4,192,768]{2,1,0:T(8,128)(2,1)} %get-tuple-element.78), channel_id=1, source_target_pairs={{0,2},{2,0},{4,6},{6,4},{1,3},{3,1},{5,7},{7,5},{8,10},{10,8},{12,... | collective-permute-start | bytes 3538952 | tf_op jit(solution)/shard_map/ppermute | solution.py:28
  129.6 52.9 %collective-permute-start.46 = (bf16[4,192,768]{2,1,0:T(8,128)(2,1)}, bf16[4,192,768]{2,1,0:T(8,128)(2,1)}, u32[]{:S(2)}, u32[]{:S(2)}) collective-permute-start(bf16[4,192,768]{2,1,0:T(8,128)(2,1)} %get-tuple-element.86), channel_id=1, source_target_pairs={{0,4},{2,6},{4,0},{6,2},{1,5},{3,7},{5,1},{7,3},{8,12},{10,14},{12... | collective-permute-start | bytes 3538952 | tf_op jit(solution)/shard_map/ppermute | solution.py:28
  173.7 43.1 %collective-permute-start.34 = (bf16[4,192,768]{2,1,0:T(8,128)(2,1)}, bf16[4,192,768]{2,1,0:T(8,128)(2,1)}, u32[]{:S(2)}, u32[]{:S(2)}) collective-permute-start(bf16[4,192,768]{2,1,0:T(8,128)(2,1)} %get-tuple-element.94), channel_id=1, source_target_pairs={{0,2},{2,0},{4,6},{6,4},{1,3},{3,1},{5,7},{7,5},{8,10},{10,8},{12,... | collective-permute-start | bytes 3538952 | tf_op jit(solution)/shard_map/ppermute | solution.py:28
  180.7 16.3 %collective-permute-start.59 = (bf16[2,192,768]{2,1,0:T(8,128)(2,1)S(1)}, bf16[2,192,768]{2,1,0:T(8,128)(2,1)S(1)}, u32[]{:S(2)}, u32[]{:S(2)}) collective-permute-start(bf16[2,192,768]{2,1,0:T(8,128)(2,1)S(1)} %get-tuple-element.76), channel_id=1, source_target_pairs={{0,8},{8,0},{16,24},{24,16},{1,9},{9,1},{17,25},{25,17},{2,10},{10... | collective-permute-start | bytes 1769480 | tf_op jit(solution)/shard_map/ppermute | solution.py:28
  184.2 30.5 %collective-permute-start.47 = (bf16[2,192,768]{2,1,0:T(8,128)(2,1)S(1)}, bf16[2,192,768]{2,1,0:T(8,128)(2,1)S(1)}, u32[]{:S(2)}, u32[]{:S(2)}) collective-permute-start(bf16[2,192,768]{2,1,0:T(8,128)(2,1)S(1)} %get-tuple-element.84), channel_id=1, source_target_pairs={{0,8},{8,0},{16,24},{24,16},{1,9},{9,1},{17,25},{25,17},{2,10},{10... | collective-permute-start | bytes 1769480 | tf_op jit(solution)/shard_map/ppermute | solution.py:28
  190.8 30.2 %collective-permute-start.20 = (bf16[256,768]{1,0:T(8,128)(2,1)S(1)}, bf16[256,768]{1,0:T(8,128)(2,1)S(1)}, u32[]{:S(2)}, u32[]{:S(2)}) collective-permute-start(bf16[256,768]{1,0:T(8,128)(2,1)S(1)} %fusion.104), channel_id=1, source_target_pairs={{0,1},{1,0},{2,3},{3,2},{4,5},{5,4},{6,7},{7,6},{8,9},{9,8},{10,11... | collective-permute-start | bytes 1179656 | tf_op jit(solution)/shard_map/ppermute | solution.py:28
  197.1 38.9 %collective-permute-start.60 = (bf16[1,192,768]{2,1,0:T(8,128)(2,1)S(1)}, bf16[1,192,768]{2,1,0:T(8,128)(2,1)S(1)}, u32[]{:S(2)}, u32[]{:S(2)}) collective-permute-start(bf16[1,192,768]{2,1,0:T(8,128)(2,1)S(1)} %get-tuple-element.99), channel_id=1, source_target_pairs={{0,16},{8,24},{16,0},{24,8},{1,17},{9,25},{17,1},{25,9},{2,18},{10... | collective-permute-start | bytes 884744 | tf_op jit(solution)/shard_map/ppermute | solution.py:28
  214.9 24.4 %collective-permute-start.48 = (bf16[1,192,768]{2,1,0:T(8,128)(2,1)S(1)}, bf16[1,192,768]{2,1,0:T(8,128)(2,1)S(1)}, u32[]{:S(2)}, u32[]{:S(2)}) collective-permute-start(bf16[1,192,768]{2,1,0:T(8,128)(2,1)S(1)} %get-tuple-element.103), channel_id=1, source_target_pairs={{0,16},{8,24},{16,0},{24,8},{1,17},{9,25},{17,1},{25,9},{2,18},{10... | collective-permute-start | bytes 884744 | tf_op jit(solution)/shard_map/ppermute | solution.py:28
  218.4 34.9 %collective-permute-start.35 = (bf16[2,192,768]{2,1,0:T(8,128)(2,1)S(1)}, bf16[2,192,768]{2,1,0:T(8,128)(2,1)S(1)}, u32[]{:S(2)}, u32[]{:S(2)}) collective-permute-start(bf16[2,192,768]{2,1,0:T(8,128)(2,1)S(1)} %get-tuple-element.92), channel_id=1, source_target_pairs={{0,8},{8,0},{16,24},{24,16},{1,9},{9,1},{17,25},{25,17},{2,10},{10... | collective-permute-start | bytes 1769480 | tf_op jit(solution)/shard_map/ppermute | solution.py:28
  234.4 11.6 %collective-permute-start.12 = (bf16[128,768]{1,0:T(8,128)(2,1)S(1)}, bf16[128,768]{1,0:T(8,128)(2,1)S(1)}, u32[]{:S(2)}, u32[]{:S(2)}) collective-permute-start(bf16[128,768]{1,0:T(8,128)(2,1)S(1)} %dynamic-slice_bitcast_fusion.4), channel_id=1, source_target_pairs={{0,2},{2,0},{4,6},{6,4},{1,3},{3,1},{5,7},{7,5},{8,10},{10,8},{12,... | collective-permute-start | bytes 589832 | tf_op jit(solution)/shard_map/ppermute | solution.py:28
  236.0 48.3 %collective-permute-start.21 = (bf16[512,768]{1,0:T(8,128)(2,1)S(1)}, bf16[512,768]{1,0:T(8,128)(2,1)S(1)}, u32[]{:S(2)}, u32[]{:S(2)}) collective-permute-start(bf16[512,768]{1,0:T(8,128)(2,1)S(1)} %fusion.72), channel_id=1, source_target_pairs={{0,1},{1,0},{2,3},{3,2},{4,5},{5,4},{6,7},{7,6},{8,9},{9,8},{10,11... | collective-permute-start | bytes 2359304 | tf_op jit(solution)/shard_map/ppermute | solution.py:28
  246.0 192.7 %collective-permute-start.52 = (bf16[4,192,768]{2,1,0:T(8,128)(2,1)}, bf16[4,192,768]{2,1,0:T(8,128)(2,1)}, u32[]{:S(2)}, u32[]{:S(2)}) collective-permute-start(bf16[4,192,768]{2,1,0:T(8,128)(2,1)} %get-tuple-element.74), channel_id=1, source_target_pairs={{0,4},{2,6},{4,0},{6,2},{1,5},{3,7},{5,1},{7,3},{8,12},{10,14},{12... | collective-permute-start | bytes 3538952 | tf_op jit(solution)/shard_map/ppermute | solution.py:28
  250.6 190.1 %collective-permute-start.40 = (bf16[4,192,768]{2,1,0:T(8,128)(2,1)}, bf16[4,192,768]{2,1,0:T(8,128)(2,1)}, u32[]{:S(2)}, u32[]{:S(2)}) collective-permute-start(bf16[4,192,768]{2,1,0:T(8,128)(2,1)} %get-tuple-element.82), channel_id=1, source_target_pairs={{0,2},{2,0},{4,6},{6,4},{1,3},{3,1},{5,7},{7,5},{8,10},{10,8},{12,... | collective-permute-start | bytes 3538952 | tf_op jit(solution)/shard_map/ppermute | solution.py:28
  251.3 28.4 %collective-permute-start.51 = (bf16[192,768]{1,0:T(8,128)(2,1)S(1)}, bf16[192,768]{1,0:T(8,128)(2,1)S(1)}, u32[]{:S(2)}, u32[]{:S(2)}) collective-permute-start(bf16[192,768]{1,0:T(8,128)(2,1)S(1)} %maximum_select_fusion.20), channel_id=1, source_target_pairs={{0,4},{2,6},{4,0},{6,2},{1,5},{3,7},{5,1},{7,3},{8,12},{10,14},{12... | collective-permute-start | bytes 884744 | tf_op jit(solution)/shard_map/ppermute | solution.py:28
  253.4 29.9 %collective-permute-start.63 = (bf16[192,768]{1,0:T(8,128)(2,1)S(1)}, bf16[192,768]{1,0:T(8,128)(2,1)S(1)}, u32[]{:S(2)}, u32[]{:S(2)}) collective-permute-start(bf16[192,768]{1,0:T(8,128)(2,1)S(1)} %maximum_select_fusion.22), channel_id=1, source_target_pairs={{0,2},{2,0},{4,6},{6,4},{1,3},{3,1},{5,7},{7,5},{8,10},{10,8},{12,... | collective-permute-start | bytes 884744 | tf_op jit(solution)/shard_map/ppermute | solution.py:28
  279.6 59.7 %collective-permute-start.36 = (bf16[1,192,768]{2,1,0:T(8,128)(2,1)}, bf16[1,192,768]{2,1,0:T(8,128)(2,1)}, u32[]{:S(2)}, u32[]{:S(2)}) collective-permute-start(bf16[1,192,768]{2,1,0:T(8,128)(2,1)} %get-tuple-element.107), channel_id=1, source_target_pairs={{0,16},{8,24},{16,0},{24,8},{1,17},{9,25},{17,1},{25,9},{2,18},{10... | collective-permute-start | bytes 884744 | tf_op jit(solution)/shard_map/ppermute | solution.py:28
  331.9 138.3 %collective-permute-start.28 = (bf16[4,192,768]{2,1,0:T(8,128)(2,1)}, bf16[4,192,768]{2,1,0:T(8,128)(2,1)}, u32[]{:S(2)}, u32[]{:S(2)}) collective-permute-start(bf16[4,192,768]{2,1,0:T(8,128)(2,1)} %get-tuple-element.90), channel_id=1, source_target_pairs={{0,4},{2,6},{4,0},{6,2},{1,5},{3,7},{5,1},{7,3},{8,12},{10,14},{12... | collective-permute-start | bytes 3538952 | tf_op jit(solution)/shard_map/ppermute | solution.py:28
  336.0 106.5 %collective-permute-start.23 = (bf16[256,768]{1,0:T(8,128)(2,1)}, bf16[256,768]{1,0:T(8,128)(2,1)}, u32[]{:S(2)}, u32[]{:S(2)}) collective-permute-start(bf16[256,768]{1,0:T(8,128)(2,1)} %fusion.166), channel_id=1, source_target_pairs={{0,1},{1,0},{2,3},{3,2},{4,5},{5,4},{6,7},{7,6},{8,9},{9,8},{10,11... | collective-permute-start | bytes 1179656 | tf_op jit(solution)/shard_map/ppermute | solution.py:28
  340.3 22.7 %collective-permute-start.37 = (bf16[1,192,384]{2,1,0:T(8,128)(2,1)S(1)}, bf16[1,192,384]{2,1,0:T(8,128)(2,1)S(1)}, u32[]{:S(2)}, u32[]{:S(2)}) collective-permute-start(bf16[1,192,384]{2,1,0:T(8,128)(2,1)S(1)} %add_convert_fusion.27), channel_id=1, source_target_pairs={{0,4},{2,6},{4,0},{6,2},{1,5},{3,7},{5,1},{7,3},{8,12},{10,14},{12... | collective-permute-start | bytes 442376 | tf_op jit(solution)/shard_map/ppermute | solution.py:28
  364.0 74.6 %collective-permute-start.38 = (bf16[192,384]{1,0:T(8,128)(2,1)S(1)}, bf16[192,384]{1,0:T(8,128)(2,1)S(1)}, u32[]{:S(2)}, u32[]{:S(2)}) collective-permute-start(bf16[192,384]{1,0:T(8,128)(2,1)S(1)} %fusion.178), channel_id=1, source_target_pairs={{0,4},{2,6},{4,0},{6,2},{1,5},{3,7},{5,1},{7,3},{8,12},{10,14},{12... | collective-permute-start | bytes 442376 | tf_op jit(solution)/shard_map/ppermute | solution.py:28
  440.7 18.6 %collective-permute-start.53 = (bf16[2,192,768]{2,1,0:T(8,128)(2,1)S(1)}, bf16[2,192,768]{2,1,0:T(8,128)(2,1)S(1)}, u32[]{:S(2)}, u32[]{:S(2)}) collective-permute-start(bf16[2,192,768]{2,1,0:T(8,128)(2,1)S(1)} %get-tuple-element.72), channel_id=1, source_target_pairs={{0,8},{8,0},{16,24},{24,16},{1,9},{9,1},{17,25},{25,17},{2,10},{10... | collective-permute-start | bytes 1769480 | tf_op jit(solution)/shard_map/ppermute | solution.py:28
  442.5 27.1 %collective-permute-start.41 = (bf16[2,192,768]{2,1,0:T(8,128)(2,1)S(1)}, bf16[2,192,768]{2,1,0:T(8,128)(2,1)S(1)}, u32[]{:S(2)}, u32[]{:S(2)}) collective-permute-start(bf16[2,192,768]{2,1,0:T(8,128)(2,1)S(1)} %get-tuple-element.80), channel_id=1, source_target_pairs={{0,8},{8,0},{16,24},{24,16},{1,9},{9,1},{17,25},{25,17},{2,10},{10... | collective-permute-start | bytes 1769480 | tf_op jit(solution)/shard_map/ppermute | solution.py:28
  459.1 15.3 %collective-permute-start.25 = (bf16[256,768]{1,0:T(8,128)(2,1)S(1)}, bf16[256,768]{1,0:T(8,128)(2,1)S(1)}, u32[]{:S(2)}, u32[]{:S(2)}) collective-permute-start(bf16[256,768]{1,0:T(8,128)(2,1)S(1)} %fusion.101), channel_id=1, source_target_pairs={{0,1},{1,0},{2,3},{3,2},{4,5},{5,4},{6,7},{7,6},{8,9},{9,8},{10,11... | collective-permute-start | bytes 1179656 | tf_op jit(solution)/shard_map/ppermute | solution.py:28
  459.5 23.3 %collective-permute-start.54 = (bf16[1,192,768]{2,1,0:T(8,128)(2,1)S(1)}, bf16[1,192,768]{2,1,0:T(8,128)(2,1)S(1)}, u32[]{:S(2)}, u32[]{:S(2)}) collective-permute-start(bf16[1,192,768]{2,1,0:T(8,128)(2,1)S(1)} %get-tuple-element.97), channel_id=1, source_target_pairs={{0,16},{8,24},{16,0},{24,8},{1,17},{9,25},{17,1},{25,9},{2,18},{10... | collective-permute-start | bytes 884744 | tf_op jit(solution)/shard_map/ppermute | solution.py:28
  469.8 19.1 %collective-permute-start.42 = (bf16[1,192,768]{2,1,0:T(8,128)(2,1)S(1)}, bf16[1,192,768]{2,1,0:T(8,128)(2,1)S(1)}, u32[]{:S(2)}, u32[]{:S(2)}) collective-permute-start(bf16[1,192,768]{2,1,0:T(8,128)(2,1)S(1)} %get-tuple-element.101), channel_id=1, source_target_pairs={{0,16},{8,24},{16,0},{24,8},{1,17},{9,25},{17,1},{25,9},{2,18},{10... | collective-permute-start | bytes 884744 | tf_op jit(solution)/shard_map/ppermute | solution.py:28
  471.8 30.3 %collective-permute-start.29 = (bf16[2,192,768]{2,1,0:T(8,128)(2,1)S(1)}, bf16[2,192,768]{2,1,0:T(8,128)(2,1)S(1)}, u32[]{:S(2)}, u32[]{:S(2)}) collective-permute-start(bf16[2,192,768]{2,1,0:T(8,128)(2,1)S(1)} %get-tuple-element.88), channel_id=1, source_target_pairs={{0,8},{8,0},{16,24},{24,16},{1,9},{9,1},{17,25},{25,17},{2,10},{10... | collective-permute-start | bytes 1769480 | tf_op jit(solution)/shard_map/ppermute | solution.py:28
  482.9 12.1 %collective-permute-start.26 = (bf16[128,768]{1,0:T(8,128)(2,1)S(1)}, bf16[128,768]{1,0:T(8,128)(2,1)S(1)}, u32[]{:S(2)}, u32[]{:S(2)}) collective-permute-start(bf16[128,768]{1,0:T(8,128)(2,1)S(1)} %dynamic-slice_bitcast_fusion.2), channel_id=1, source_target_pairs={{0,2},{2,0},{4,6},{6,4},{1,3},{3,1},{5,7},{7,5},{8,10},{10,8},{12,... | collective-permute-start | bytes 589832 | tf_op jit(solution)/shard_map/ppermute | solution.py:28
  501.4 19.1 %collective-permute-start.45 = (bf16[192,768]{1,0:T(8,128)(2,1)S(1)}, bf16[192,768]{1,0:T(8,128)(2,1)S(1)}, u32[]{:S(2)}, u32[]{:S(2)}) collective-permute-start(bf16[192,768]{1,0:T(8,128)(2,1)S(1)} %maximum_select_fusion.19), channel_id=1, source_target_pairs={{0,2},{2,0},{4,6},{6,4},{1,3},{3,1},{5,7},{7,5},{8,10},{10,8},{12,... | collective-permute-start | bytes 884744 | tf_op jit(solution)/shard_map/ppermute | solution.py:28
  502.3 12.3 %collective-permute-start.30 = (bf16[1,192,768]{2,1,0:T(8,128)(2,1)S(1)}, bf16[1,192,768]{2,1,0:T(8,128)(2,1)S(1)}, u32[]{:S(2)}, u32[]{:S(2)}) collective-permute-start(bf16[1,192,768]{2,1,0:T(8,128)(2,1)S(1)} %get-tuple-element.105), channel_id=1, source_target_pairs={{0,16},{8,24},{16,0},{24,8},{1,17},{9,25},{17,1},{25,9},{2,18},{10... | collective-permute-start | bytes 884744 | tf_op jit(solution)/shard_map/ppermute | solution.py:28
  (142 other events, 946.5 us)

commit v2 on v1

--- a/solution.py
+++ b/solution.py
@@ -117,6 +117,13 @@
             jnp.concatenate([other, total], axis=1),
         )
     return total
+
+
+def sum_everywhere(value):
+    for axis in ("seq", "dp"):
+        for bit in range(bits_of(axis)):
+            value = value + swap(value, axis, 1 << bit)
+    return value
 
 
 def split_heads(value):
@@ -273,15 +280,20 @@
         total_half = total_half + swap(half_sum(back_kv[j]).astype(bf16), "seq", 2 * j).astype(f32)
     back_total = share_halves(total_half.astype(bf16))
     grad_inputs = grad_attended + back_total.astype(f32)
-    small = (
-        jnp.stack(
-            [jnp.sum(grad_query.astype(f32), axis=0), jnp.sum(grad_value.astype(f32), axis=0)]
-        ),
-        grad_bias_out,
-        jnp.stack([gain_one, gain_two]),
-        jnp.stack([shift_one, shift_two]),
-        grad_bias_up,
-        grad_bias_down,
+    small = jnp.stack(
+        [
+            jnp.concatenate(
+                [jnp.sum(grad_query.astype(f32), axis=0), jnp.sum(grad_value.astype(f32), axis=0)]
+            ),
+            grad_bias_out,
+            gain_one,
+            gain_two,
+            shift_one,
+            shift_two,
+            grad_bias_up[: grad_bias_up.shape[0] // 2],
+            grad_bias_up[grad_bias_up.shape[0] // 2 :],
+            grad_bias_down,
+        ]
     )
     return (grad_inputs, small, (attn_sum, up_sum, down_sum))
 
@@ -370,8 +382,13 @@
         grad_hidden_one, saved_one, same, first, (down_up, up_down, down_up)
     )
     tokens_grad = send_back(grad_tokens)
-    small = jax.tree.map(stack_pair, small_one, small_two)
-    qv_sum, out_bias_sum, gain_sum, shift_sum, up_bias_sum, down_bias_sum = lax.psum(small, ("dp", "seq"))
+    small = sum_everywhere(jnp.stack([small_one, small_two]))
+    halves = width // 2
+    qv_sum = small[:, 0].reshape(2, 2, halves)
+    out_bias_sum = small[:, 1]
+    gain_sum, shift_sum = small[:, 2:4], small[:, 4:6]
+    up_bias_sum = small[:, 6:8].reshape(2, 2 * width)
+    down_bias_sum = small[:, 8]
 
     def attn_parts(total):
         quarter = total.shape[1] // 4

time: 536 us -> 484 us (0.903); the launches traced: 535 us -> 477 us
  blocking collectives: 72.8 us -> 0 us
  starting transfers between devices: 50.6 us -> 65 us
  waiting for transfers between devices: 171 us -> 161 us
  other arithmetic: 69.4 us -> 75.9 us
    psum x1 -> x0, blocking collectives: 72.8 us -> none  [local(): lax.psum(small, ('dp', 'seq'))]
    ppermute x64 -> x68, starting transfers between devices: 50.6 us -> 65 us  [swap(): return lax.ppermute(value, axis, [(i, i ^ mask) for i in range(count)])]
    ppermute x64 -> x68, waiting for transfers between devices: 171 us -> 161 us  [swap(): return lax.ppermute(value, axis, [(i, i ^ mask) for i in range(count)])]
    unnamed x221 -> x251, local copies, waits for them, and re-layouts: 8.96 us -> 11.1 us
  transfers between devices with their start and end apart: 64 -> 68, of which waited for: 33 -> 33; matrix products, arithmetic and copies ran while one was open for 32% -> 38% of each run, Pallas kernels for 0% -> 0%
where the time goes in v2:
time: 484 us; the launch traced here: 477 us
  waiting for transfers between devices  161 us (33%)
  matrix products  127 us (26%)
  other arithmetic  75.9 us (16%)
  starting transfers between devices  65 us (13%)
  local copies, waits for them, and re-layouts  44.4 us (9%)
    ppermute x68, waiting for transfers between devices, swap(): return lax.ppermute(value, axis, [(i, i ^ mask) for i in range(count)])  161 us
    ppermute x68, starting transfers between devices, swap(): return lax.ppermute(value, axis, [(i, i ^ mask) for i in range(count)])  65 us
    dot_general x12, matrix products, dot_nn(): lax.dot_general(left, right, (((1,), (0,)), ((), ())), preferred_element_...  42.4 us
    dot_general x12, matrix products, dot_nt(): lax.dot_general(left, right, (((1,), (1,)), ((), ())), preferred_element_...  25.5 us
    convert_element_type x18, other arithmetic, add_low(): return (left.astype(f32) + right.astype(f32)).astype(bf16)  16.8 us
    dot_general x12, matrix products, dot_tn(): lax.dot_general(left, right, (((0,), (0,)), ((), ())), preferred_element_...  16.3 us
    dot_general x2, matrix products, attend_back(): jnp.einsum('qhd,khd->hqk', grad_context, value_all, preferred_element_typ...  14.5 us
    convert_element_type x2, other arithmetic, attend_back(): grad_score = grad_score.astype(bf16)  14.2 us
  transfers between devices with their start and end apart: 68, of which 33 were waited for; matrix products, arithmetic and copies ran while one was open for 38% of the time, Pallas kernels for 0%

profile of v2, /device:TPU:0, one launch (start us, length us, event | category | flops | bytes accessed | tf_op | source)
XLA Modules:
  0.0 476.7 jit_solution(8351707513444142440)
XLA Ops:
  1.9 4.0 collective-permute-start.4
  6.8 8.2 %collective-permute-done.2 = bf16[128,768]{1,0:T(8,128)(2,1)S(1)} collective-permute-done((bf16[128,768]{1,0:T(8,128)(2,1)S(1)}, bf16[128,768]{1,0:T(8,128)(2,1)S(1)}, u32[]{:S(2)}, u32[]{:S(2)}) %collective-permute-start.2) | collective-permute-done | bytes 196640 | tf_op jit(solution)/shard_map/ppermute | solution.py:28
  24.0 3.6 fusion
  29.7 4.7 fusion.97
  38.2 9.5 %fusion.14 = (bf16[512,1536]{1,0:T(8,128)(2,1)S(1)}, f32[512,1536]{1,0:T(8,128)}) fusion(f32[1536]{0:T(1024)S(1)} %get-tuple-element.60, bf16[2,768,1536]{2,1,0:T(8,128)(2,1)S(1)} %bitcast.508, f32[512,768]{1,0:T(8,128)S(1)} %get-tuple-element.88, f32[768]{0:T(1024)S(1)} %get-tuple-element.58, f32[768]{0:T(1024)S(1)} %get-tuple-element.173, ...), kind=kOutput, calls=%fused_computation.36 | convolution fusion | flops 1261830144 | bytes 8671232 | tf_op jit(solution)/shard_map/dot_general | solution.py:15
  54.8 9.5 %collective-permute-done.8 = bf16[256,768]{1,0:T(8,128)(2,1)S(1)} collective-permute-done((bf16[256,768]{1,0:T(8,128)(2,1)S(1)}, bf16[256,768]{1,0:T(8,128)(2,1)S(1)}, u32[]{:S(2)}, u32[]{:S(2)}) %collective-permute-start.8) | collective-permute-done | bytes 393248 | tf_op jit(solution)/shard_map/ppermute | solution.py:28
  64.3 13.3 %fusion.93 = bf16[512,384]{0,1:T(8,128)(2,1)S(1)} fusion(bf16[512,768]{1,0:T(8,128)(2,1)S(1)} %fusion.98, bf16[2,3,768,384]{3,2,1,0:T(8,128)(2,1)S(1)} %copy-done.20, f32[384]{0:T(512)S(1)} %get-tuple-element.66), kind=kOutput, calls=%fused_computation.187 | convolution fusion | flops 302383104 | bytes 1771520 | tf_op jit(solution)/shard_map/dot_general | solution.py:15
  82.0 3.6 fusion.1
  86.6 4.3 fusion.96
  95.0 9.6 %fusion.17 = (bf16[512,1536]{1,0:T(8,128)(2,1)S(1)}, f32[512,1536]{1,0:T(8,128)}) fusion(f32[1536]{0:T(1024)S(1)} %get-tuple-element.61, bf16[2,768,1536]{2,1,0:T(8,128)(2,1)S(1)} %bitcast.508, f32[512,768]{1,0:T(8,128)S(1)} %get-tuple-element.84, f32[768]{0:T(1024)S(1)} %get-tuple-element.59, f32[768]{0:T(1024)S(1)} %get-tuple-element.172, ...), kind=kOutput, calls=%fused_computation.39 | convolution fusion | flops 1261830144 | bytes 8671232 | tf_op jit(solution)/shard_map/dot_general | solution.py:15
  117.0 4.0 convert_reduce_fusion
  139.0 7.4 %multiply_reduce_fusion.1 = (f32[6,512]{1,0:T(8,128)S(1)}, f32[6,512,1024]{2,1,0:T(8,128)}) fusion(f32[6,512,1024]{2,1,0:T(8,128)S(1)} %bitcast.392, f32[6,512]{1,0:T(8,128)S(1)} %log_add_fusion.1, pred[512,1024]{1,0:T(8,128)(4,1)S(1)} %broadcast_compare_fusion, bf16[512,6,64]{0,2,1:T(8,128)(2,1)S(1)} %bitcast.450, bf16[1024,6,64]{0,2,1:T(8,128)(2,1)S(1)} %bitcast.462), kind=kOutput, calls=%fused_computation.4 | convolution fusion | flops 418378752 | bytes 26894336 | tf_op jit(solution)/shard_map/qhd,khd->hqk/dot_general | solution.py:153
  146.4 6.9 %multiply_convert_fusion.1 = bf16[6,512,1024]{2,1,0:T(8,128)(2,1)S(1)} fusion(f32[6,512,1024]{2,1,0:T(8,128)} %get-tuple-element.157, f32[6,512,1024]{2,1,0:T(8,128)S(1)} %bitcast.392, f32[6,512]{1,0:T(8,128)S(1)} %get-tuple-element.156, f32[6,512]{1,0:T(8,128)S(1)} %log_add_fusion.1, pred[512,1024]{1,0:T(8,128)(4,1)S(1)} %broadcast_compare_fusion), kind=kLoop, calls=%fused_computation.3 | loop fusion | flops 18874368 | bytes 32006144 | tf_op jit(solution)/shard_map/convert_element_type | solution.py:156
  165.8 4.3 copy.37
  186.5 3.5 collective-permute-done.19
  194.8 3.5 collective-permute-done.63
  202.2 13.7 %collective-permute-done.51 = bf16[2,192,768]{2,1,0:T(8,128)(2,1)} collective-permute-done((bf16[2,192,768]{2,1,0:T(8,128)(2,1)}, bf16[2,192,768]{2,1,0:T(8,128)(2,1)}, u32[]{:S(2)}, u32[]{:S(2)}) %collective-permute-start.51) | collective-permute-done | bytes 589856 | tf_op jit(solution)/shard_map/ppermute | solution.py:28
  256.7 26.9 %collective-permute-done.55 = bf16[192,768]{1,0:T(8,128)(2,1)S(1)} collective-permute-done((bf16[192,768]{1,0:T(8,128)(2,1)S(1)}, bf16[192,768]{1,0:T(8,128)(2,1)S(1)}, u32[]{:S(2)}, u32[]{:S(2)}) %collective-permute-start.55) | collective-permute-done | bytes 294944 | tf_op jit(solution)/shard_map/ppermute | solution.py:28
  290.3 3.9 convert_reduce_fusion.3
  294.2 7.1 %multiply_reduce_fusion = (f32[6,512]{1,0:T(8,128)S(1)}, f32[6,512,1024]{2,1,0:T(8,128)}) fusion(f32[6,512,1024]{2,1,0:T(8,128)S(1)} %bitcast.390, f32[6,512]{1,0:T(8,128)S(1)} %copy-done.66, pred[512,1024]{1,0:T(8,128)(4,1)S(1)} %broadcast_compare_fusion, bf16[512,6,64]{0,2,1:T(8,128)(2,1)S(1)} %bitcast.452, bf16[1024,6,64]{0,2,1:T(8,128)(2,1)S(1)} %bitcast.460), kind=kOutput, calls=%fused_computation.1 | convolution fusion | flops 418378752 | bytes 26894336 | tf_op jit(solution)/shard_map/qhd,khd->hqk/dot_general | solution.py:153
  301.3 7.3 %multiply_convert_fusion = bf16[6,512,1024]{2,1,0:T(8,128)(2,1)S(1)} fusion(f32[6,512,1024]{2,1,0:T(8,128)} %get-tuple-element.159, f32[6,512,1024]{2,1,0:T(8,128)S(1)} %bitcast.390, f32[6,512]{1,0:T(8,128)S(1)} %get-tuple-element.158, f32[6,512]{1,0:T(8,128)S(1)} %copy-done.66, pred[512,1024]{1,0:T(8,128)(4,1)S(1)} %broadcast_compare_fusion), kind=kLoop, calls=%fused_computation | loop fusion | flops 18874368 | bytes 32006144 | tf_op jit(solution)/shard_map/convert_element_type | solution.py:156
  314.3 3.8 fusion.137
  324.7 4.5 copy.36
  356.1 15.7 %collective-permute-done.37 = bf16[1,192,384]{2,1,0:T(8,128)(2,1)S(1)} collective-permute-done((bf16[1,192,384]{2,1,0:T(8,128)(2,1)S(1)}, bf16[1,192,384]{2,1,0:T(8,128)(2,1)S(1)}, u32[]{:S(2)}, u32[]{:S(2)}) %collective-permute-start.37) | collective-permute-done | bytes 147488 | tf_op jit(solution)/shard_map/ppermute | solution.py:28
  389.1 9.3 %collective-permute-done.24 = bf16[256,768]{1,0:T(8,128)(2,1)S(1)} collective-permute-done((bf16[256,768]{1,0:T(8,128)(2,1)S(1)}, bf16[256,768]{1,0:T(8,128)(2,1)S(1)}, u32[]{:S(2)}, u32[]{:S(2)}) %collective-permute-start.24) | collective-permute-done | bytes 393248 | tf_op jit(solution)/shard_map/ppermute | solution.py:28
  401.6 14.0 %collective-permute-done.45 = bf16[2,192,768]{2,1,0:T(8,128)(2,1)S(1)} collective-permute-done((bf16[2,192,768]{2,1,0:T(8,128)(2,1)S(1)}, bf16[2,192,768]{2,1,0:T(8,128)(2,1)S(1)}, u32[]{:S(2)}, u32[]{:S(2)}) %collective-permute-start.45) | collective-permute-done | bytes 589856 | tf_op jit(solution)/shard_map/ppermute | solution.py:28
  422.9 8.2 %collective-permute-done.46 = bf16[1,192,768]{2,1,0:T(8,128)(2,1)S(1)} collective-permute-done((bf16[1,192,768]{2,1,0:T(8,128)(2,1)S(1)}, bf16[1,192,768]{2,1,0:T(8,128)(2,1)S(1)}, u32[]{:S(2)}, u32[]{:S(2)}) %collective-permute-start.46) | collective-permute-done | bytes 294944 | tf_op jit(solution)/shard_map/ppermute | solution.py:28
  433.5 3.4 collective-permute-done.47
  439.4 3.5 collective-permute-done.48
  448.7 8.0 %collective-permute-done.30 = bf16[1,192,768]{2,1,0:T(8,128)(2,1)S(1)} collective-permute-done((bf16[1,192,768]{2,1,0:T(8,128)(2,1)S(1)}, bf16[1,192,768]{2,1,0:T(8,128)(2,1)S(1)}, u32[]{:S(2)}, u32[]{:S(2)}) %collective-permute-start.30) | collective-permute-done | bytes 294944 | tf_op jit(solution)/shard_map/ppermute | solution.py:28
  463.1 4.1 collective-permute-done.32
  469.9 4.1 collective-permute-done.33
  (595 shorter events, 235.3 us)
Async XLA Ops:
  1.9 13.5 %collective-permute-start.4 = (bf16[128,768]{1,0:T(8,128)(2,1)S(1)}, bf16[128,768]{1,0:T(8,128)(2,1)S(1)}, u32[]{:S(2)}, u32[]{:S(2)}) collective-permute-start(bf16[128,768]{1,0:T(8,128)(2,1)S(1)} %dynamic-slice_bitcast_fusion.6), channel_id=1, source_target_pairs={{0,6},{2,4},{4,2},{6,0},{1,7},{3,5},{5,3},{7,1},{8,14},{10,12},{12... | collective-permute-start | bytes 589832 | tf_op jit(solution)/shard_map/ppermute | solution.py:28
  64.3 13.4 %collective-permute-start.9 = (bf16[256,768]{1,0:T(8,128)(2,1)S(1)}, bf16[256,768]{1,0:T(8,128)(2,1)S(1)}, u32[]{:S(2)}, u32[]{:S(2)}) collective-permute-start(bf16[256,768]{1,0:T(8,128)(2,1)S(1)} %collective-permute-done.8), channel_id=1, source_target_pairs={{0,1},{1,0},{2,3},{3,2},{4,5},{5,4},{6,7},{7,6},{8,9},{9,8},{10,11... | collective-permute-start | bytes 1179656 | tf_op jit(solution)/shard_map/ppermute | solution.py:28
  92.2 15.2 %collective-permute-start.14 = (bf16[128,768]{1,0:T(8,128)(2,1)S(1)}, bf16[128,768]{1,0:T(8,128)(2,1)S(1)}, u32[]{:S(2)}, u32[]{:S(2)}) collective-permute-start(bf16[128,768]{1,0:T(8,128)(2,1)S(1)} %dynamic-slice_bitcast_fusion.3), channel_id=1, source_target_pairs={{0,2},{2,0},{4,6},{6,4},{1,3},{3,1},{5,7},{7,5},{8,10},{10,8},{12,... | collective-permute-start | bytes 589832 | tf_op jit(solution)/shard_map/ppermute | solution.py:28
  126.0 53.2 %collective-permute-start.62 = (bf16[4,192,768]{2,1,0:T(8,128)(2,1)}, bf16[4,192,768]{2,1,0:T(8,128)(2,1)}, u32[]{:S(2)}, u32[]{:S(2)}) collective-permute-start(bf16[4,192,768]{2,1,0:T(8,128)(2,1)} %get-tuple-element.96), channel_id=1, source_target_pairs={{0,2},{2,0},{4,6},{6,4},{1,3},{3,1},{5,7},{7,5},{8,10},{10,8},{12,... | collective-permute-start | bytes 3538952 | tf_op jit(solution)/shard_map/ppermute | solution.py:28
  130.9 52.4 %collective-permute-start.50 = (bf16[4,192,768]{2,1,0:T(8,128)(2,1)}, bf16[4,192,768]{2,1,0:T(8,128)(2,1)}, u32[]{:S(2)}, u32[]{:S(2)}) collective-permute-start(bf16[4,192,768]{2,1,0:T(8,128)(2,1)} %get-tuple-element.104), channel_id=1, source_target_pairs={{0,4},{2,6},{4,0},{6,2},{1,5},{3,7},{5,1},{7,3},{8,12},{10,14},{12... | collective-permute-start | bytes 3538952 | tf_op jit(solution)/shard_map/ppermute | solution.py:28
  174.2 44.7 %collective-permute-start.34 = (bf16[4,192,768]{2,1,0:T(8,128)(2,1)}, bf16[4,192,768]{2,1,0:T(8,128)(2,1)}, u32[]{:S(2)}, u32[]{:S(2)}) collective-permute-start(bf16[4,192,768]{2,1,0:T(8,128)(2,1)} %get-tuple-element.112), channel_id=1, source_target_pairs={{0,2},{2,0},{4,6},{6,4},{1,3},{3,1},{5,7},{7,5},{8,10},{10,8},{12,... | collective-permute-start | bytes 3538952 | tf_op jit(solution)/shard_map/ppermute | solution.py:28
  181.7 16.5 %collective-permute-start.63 = (bf16[2,192,768]{2,1,0:T(8,128)(2,1)}, bf16[2,192,768]{2,1,0:T(8,128)(2,1)}, u32[]{:S(2)}, u32[]{:S(2)}) collective-permute-start(bf16[2,192,768]{2,1,0:T(8,128)(2,1)} %get-tuple-element.94), channel_id=1, source_target_pairs={{0,8},{8,0},{16,24},{24,16},{1,9},{9,1},{17,25},{25,17},{2,10},{10... | collective-permute-start | bytes 1769480 | tf_op jit(solution)/shard_map/ppermute | solution.py:28
  185.9 30.0 %collective-permute-start.51 = (bf16[2,192,768]{2,1,0:T(8,128)(2,1)}, bf16[2,192,768]{2,1,0:T(8,128)(2,1)}, u32[]{:S(2)}, u32[]{:S(2)}) collective-permute-start(bf16[2,192,768]{2,1,0:T(8,128)(2,1)} %get-tuple-element.102), channel_id=1, source_target_pairs={{0,8},{8,0},{16,24},{24,16},{1,9},{9,1},{17,25},{25,17},{2,10},{10... | collective-permute-start | bytes 1769480 | tf_op jit(solution)/shard_map/ppermute | solution.py:28
  192.2 30.9 %collective-permute-start.20 = (bf16[256,768]{1,0:T(8,128)(2,1)}, bf16[256,768]{1,0:T(8,128)(2,1)}, u32[]{:S(2)}, u32[]{:S(2)}) collective-permute-start(bf16[256,768]{1,0:T(8,128)(2,1)} %fusion.104), channel_id=1, source_target_pairs={{0,1},{1,0},{2,3},{3,2},{4,5},{5,4},{6,7},{7,6},{8,9},{9,8},{10,11... | collective-permute-start | bytes 1179656 | tf_op jit(solution)/shard_map/ppermute | solution.py:28
  199.5 38.5 %collective-permute-start.64 = (bf16[1,192,768]{2,1,0:T(8,128)(2,1)S(1)}, bf16[1,192,768]{2,1,0:T(8,128)(2,1)S(1)}, u32[]{:S(2)}, u32[]{:S(2)}) collective-permute-start(bf16[1,192,768]{2,1,0:T(8,128)(2,1)S(1)} %get-tuple-element.117), channel_id=1, source_target_pairs={{0,16},{8,24},{16,0},{24,8},{1,17},{9,25},{17,1},{25,9},{2,18},{10... | collective-permute-start | bytes 884744 | tf_op jit(solution)/shard_map/ppermute | solution.py:28
  217.1 23.7 %collective-permute-start.52 = (bf16[1,192,768]{2,1,0:T(8,128)(2,1)S(1)}, bf16[1,192,768]{2,1,0:T(8,128)(2,1)S(1)}, u32[]{:S(2)}, u32[]{:S(2)}) collective-permute-start(bf16[1,192,768]{2,1,0:T(8,128)(2,1)S(1)} %get-tuple-element.121), channel_id=1, source_target_pairs={{0,16},{8,24},{16,0},{24,8},{1,17},{9,25},{17,1},{25,9},{2,18},{10... | collective-permute-start | bytes 884744 | tf_op jit(solution)/shard_map/ppermute | solution.py:28
  220.6 34.1 %collective-permute-start.35 = (bf16[2,192,768]{2,1,0:T(8,128)(2,1)S(1)}, bf16[2,192,768]{2,1,0:T(8,128)(2,1)S(1)}, u32[]{:S(2)}, u32[]{:S(2)}) collective-permute-start(bf16[2,192,768]{2,1,0:T(8,128)(2,1)S(1)} %get-tuple-element.110), channel_id=1, source_target_pairs={{0,8},{8,0},{16,24},{24,16},{1,9},{9,1},{17,25},{25,17},{2,10},{10... | collective-permute-start | bytes 1769480 | tf_op jit(solution)/shard_map/ppermute | solution.py:28
  236.4 12.3 %collective-permute-start.12 = (bf16[128,768]{1,0:T(8,128)(2,1)S(1)}, bf16[128,768]{1,0:T(8,128)(2,1)S(1)}, u32[]{:S(2)}, u32[]{:S(2)}) collective-permute-start(bf16[128,768]{1,0:T(8,128)(2,1)S(1)} %dynamic-slice_bitcast_fusion.4), channel_id=1, source_target_pairs={{0,2},{2,0},{4,6},{6,4},{1,3},{3,1},{5,7},{7,5},{8,10},{10,8},{12,... | collective-permute-start | bytes 589832 | tf_op jit(solution)/shard_map/ppermute | solution.py:28
  248.6 37.2 %collective-permute-start.21 = (bf16[512,768]{1,0:T(8,128)(2,1)S(1)}, bf16[512,768]{1,0:T(8,128)(2,1)S(1)}, u32[]{:S(2)}, u32[]{:S(2)}) collective-permute-start(bf16[512,768]{1,0:T(8,128)(2,1)S(1)} %fusion.72), channel_id=1, source_target_pairs={{0,1},{1,0},{2,3},{3,2},{4,5},{5,4},{6,7},{7,6},{8,9},{9,8},{10,11... | collective-permute-start | bytes 2359304 | tf_op jit(solution)/shard_map/ppermute | solution.py:28
  248.7 129.4 %collective-permute-start.56 = (bf16[4,192,768]{2,1,0:T(8,128)(2,1)}, bf16[4,192,768]{2,1,0:T(8,128)(2,1)}, u32[]{:S(2)}, u32[]{:S(2)}) collective-permute-start(bf16[4,192,768]{2,1,0:T(8,128)(2,1)} %get-tuple-element.92), channel_id=1, source_target_pairs={{0,4},{2,6},{4,0},{6,2},{1,5},{3,7},{5,1},{7,3},{8,12},{10,14},{12... | collective-permute-start | bytes 3538952 | tf_op jit(solution)/shard_map/ppermute | solution.py:28
  251.4 129.7 %collective-permute-start.44 = (bf16[4,192,768]{2,1,0:T(8,128)(2,1)}, bf16[4,192,768]{2,1,0:T(8,128)(2,1)}, u32[]{:S(2)}, u32[]{:S(2)}) collective-permute-start(bf16[4,192,768]{2,1,0:T(8,128)(2,1)} %get-tuple-element.100), channel_id=1, source_target_pairs={{0,2},{2,0},{4,6},{6,4},{1,3},{3,1},{5,7},{7,5},{8,10},{10,8},{12,... | collective-permute-start | bytes 3538952 | tf_op jit(solution)/shard_map/ppermute | solution.py:28
  252.2 31.4 %collective-permute-start.55 = (bf16[192,768]{1,0:T(8,128)(2,1)S(1)}, bf16[192,768]{1,0:T(8,128)(2,1)S(1)}, u32[]{:S(2)}, u32[]{:S(2)}) collective-permute-start(bf16[192,768]{1,0:T(8,128)(2,1)S(1)} %maximum_select_fusion.20), channel_id=1, source_target_pairs={{0,4},{2,6},{4,0},{6,2},{1,5},{3,7},{5,1},{7,3},{8,12},{10,14},{12... | collective-permute-start | bytes 884744 | tf_op jit(solution)/shard_map/ppermute | solution.py:28
  254.6 30.2 %collective-permute-start.67 = (bf16[192,768]{1,0:T(8,128)(2,1)S(1)}, bf16[192,768]{1,0:T(8,128)(2,1)S(1)}, u32[]{:S(2)}, u32[]{:S(2)}) collective-permute-start(bf16[192,768]{1,0:T(8,128)(2,1)S(1)} %maximum_select_fusion.22), channel_id=1, source_target_pairs={{0,2},{2,0},{4,6},{6,4},{1,3},{3,1},{5,7},{7,5},{8,10},{10,8},{12,... | collective-permute-start | bytes 884744 | tf_op jit(solution)/shard_map/ppermute | solution.py:28
  283.6 64.7 %collective-permute-start.36 = (bf16[1,192,768]{2,1,0:T(8,128)(2,1)}, bf16[1,192,768]{2,1,0:T(8,128)(2,1)}, u32[]{:S(2)}, u32[]{:S(2)}) collective-permute-start(bf16[1,192,768]{2,1,0:T(8,128)(2,1)} %get-tuple-element.125), channel_id=1, source_target_pairs={{0,16},{8,24},{16,0},{24,8},{1,17},{9,25},{17,1},{25,9},{2,18},{10... | collective-permute-start | bytes 884744 | tf_op jit(solution)/shard_map/ppermute | solution.py:28
  341.4 74.8 %collective-permute-start.28 = (bf16[4,192,768]{2,1,0:T(8,128)(2,1)}, bf16[4,192,768]{2,1,0:T(8,128)(2,1)}, u32[]{:S(2)}, u32[]{:S(2)}) collective-permute-start(bf16[4,192,768]{2,1,0:T(8,128)(2,1)} %get-tuple-element.108), channel_id=1, source_target_pairs={{0,4},{2,6},{4,0},{6,2},{1,5},{3,7},{5,1},{7,3},{8,12},{10,14},{12... | collective-permute-start | bytes 3538952 | tf_op jit(solution)/shard_map/ppermute | solution.py:28
  348.3 34.9 %collective-permute-start.23 = (bf16[256,768]{1,0:T(8,128)(2,1)}, bf16[256,768]{1,0:T(8,128)(2,1)}, u32[]{:S(2)}, u32[]{:S(2)}) collective-permute-start(bf16[256,768]{1,0:T(8,128)(2,1)} %fusion.166), channel_id=1, source_target_pairs={{0,1},{1,0},{2,3},{3,2},{4,5},{5,4},{6,7},{7,6},{8,9},{9,8},{10,11... | collective-permute-start | bytes 1179656 | tf_op jit(solution)/shard_map/ppermute | solution.py:28
  355.0 16.9 %collective-permute-start.37 = (bf16[1,192,384]{2,1,0:T(8,128)(2,1)S(1)}, bf16[1,192,384]{2,1,0:T(8,128)(2,1)S(1)}, u32[]{:S(2)}, u32[]{:S(2)}) collective-permute-start(bf16[1,192,384]{2,1,0:T(8,128)(2,1)S(1)} %add_convert_fusion.27), channel_id=1, source_target_pairs={{0,4},{2,6},{4,0},{6,2},{1,5},{3,7},{5,1},{7,3},{8,12},{10,14},{12... | collective-permute-start | bytes 442376 | tf_op jit(solution)/shard_map/ppermute | solution.py:28
  381.0 17.6 %collective-permute-start.57 = (bf16[2,192,768]{2,1,0:T(8,128)(2,1)S(1)}, bf16[2,192,768]{2,1,0:T(8,128)(2,1)S(1)}, u32[]{:S(2)}, u32[]{:S(2)}) collective-permute-start(bf16[2,192,768]{2,1,0:T(8,128)(2,1)S(1)} %get-tuple-element.90), channel_id=1, source_target_pairs={{0,8},{8,0},{16,24},{24,16},{1,9},{9,1},{17,25},{25,17},{2,10},{10... | collective-permute-start | bytes 1769480 | tf_op jit(solution)/shard_map/ppermute | solution.py:28
  383.3 32.3 %collective-permute-start.45 = (bf16[2,192,768]{2,1,0:T(8,128)(2,1)S(1)}, bf16[2,192,768]{2,1,0:T(8,128)(2,1)S(1)}, u32[]{:S(2)}, u32[]{:S(2)}) collective-permute-start(bf16[2,192,768]{2,1,0:T(8,128)(2,1)S(1)} %get-tuple-element.98), channel_id=1, source_target_pairs={{0,8},{8,0},{16,24},{24,16},{1,9},{9,1},{17,25},{25,17},{2,10},{10... | collective-permute-start | bytes 1769480 | tf_op jit(solution)/shard_map/ppermute | solution.py:28
  398.5 21.8 %collective-permute-start.25 = (bf16[256,768]{1,0:T(8,128)(2,1)S(1)}, bf16[256,768]{1,0:T(8,128)(2,1)S(1)}, u32[]{:S(2)}, u32[]{:S(2)}) collective-permute-start(bf16[256,768]{1,0:T(8,128)(2,1)S(1)} %fusion.101), channel_id=1, source_target_pairs={{0,1},{1,0},{2,3},{3,2},{4,5},{5,4},{6,7},{7,6},{8,9},{9,8},{10,11... | collective-permute-start | bytes 1179656 | tf_op jit(solution)/shard_map/ppermute | solution.py:28
  398.9 21.8 %collective-permute-start.58 = (bf16[1,192,768]{2,1,0:T(8,128)(2,1)S(1)}, bf16[1,192,768]{2,1,0:T(8,128)(2,1)S(1)}, u32[]{:S(2)}, u32[]{:S(2)}) collective-permute-start(bf16[1,192,768]{2,1,0:T(8,128)(2,1)S(1)} %get-tuple-element.115), channel_id=1, source_target_pairs={{0,16},{8,24},{16,0},{24,8},{1,17},{9,25},{17,1},{25,9},{2,18},{10... | collective-permute-start | bytes 884744 | tf_op jit(solution)/shard_map/ppermute | solution.py:28
  415.7 15.4 %collective-permute-start.46 = (bf16[1,192,768]{2,1,0:T(8,128)(2,1)S(1)}, bf16[1,192,768]{2,1,0:T(8,128)(2,1)S(1)}, u32[]{:S(2)}, u32[]{:S(2)}) collective-permute-start(bf16[1,192,768]{2,1,0:T(8,128)(2,1)S(1)} %get-tuple-element.119), channel_id=1, source_target_pairs={{0,16},{8,24},{16,0},{24,8},{1,17},{9,25},{17,1},{25,9},{2,18},{10... | collective-permute-start | bytes 884744 | tf_op jit(solution)/shard_map/ppermute | solution.py:28
  417.8 26.6 %collective-permute-start.29 = (bf16[2,192,768]{2,1,0:T(8,128)(2,1)S(1)}, bf16[2,192,768]{2,1,0:T(8,128)(2,1)S(1)}, u32[]{:S(2)}, u32[]{:S(2)}) collective-permute-start(bf16[2,192,768]{2,1,0:T(8,128)(2,1)S(1)} %get-tuple-element.106), channel_id=1, source_target_pairs={{0,8},{8,0},{16,24},{24,16},{1,9},{9,1},{17,25},{25,17},{2,10},{10... | collective-permute-start | bytes 1769480 | tf_op jit(solution)/shard_map/ppermute | solution.py:28
  420.8 11.5 %collective-permute-start.59 = (bf16[1,192,384]{2,1,0:T(8,128)(2,1)S(1)}, bf16[1,192,384]{2,1,0:T(8,128)(2,1)S(1)}, u32[]{:S(2)}, u32[]{:S(2)}) collective-permute-start(bf16[1,192,384]{2,1,0:T(8,128)(2,1)S(1)} %add_convert_fusion.18), channel_id=1, source_target_pairs={{0,2},{2,0},{4,6},{6,4},{1,3},{3,1},{5,7},{7,5},{8,10},{10,8},{12,... | collective-permute-start | bytes 442376 | tf_op jit(solution)/shard_map/ppermute | solution.py:28
  421.9 16.2 %collective-permute-start.26 = (bf16[128,768]{1,0:T(8,128)(2,1)S(1)}, bf16[128,768]{1,0:T(8,128)(2,1)S(1)}, u32[]{:S(2)}, u32[]{:S(2)}) collective-permute-start(bf16[128,768]{1,0:T(8,128)(2,1)S(1)} %dynamic-slice_bitcast_fusion.2), channel_id=1, source_target_pairs={{0,2},{2,0},{4,6},{6,4},{1,3},{3,1},{5,7},{7,5},{8,10},{10,8},{12,... | collective-permute-start | bytes 589832 | tf_op jit(solution)/shard_map/ppermute | solution.py:28
  443.1 19.9 %collective-permute-start.49 = (bf16[192,768]{1,0:T(8,128)(2,1)S(1)}, bf16[192,768]{1,0:T(8,128)(2,1)S(1)}, u32[]{:S(2)}, u32[]{:S(2)}) collective-permute-start(bf16[192,768]{1,0:T(8,128)(2,1)S(1)} %maximum_select_fusion.19), channel_id=1, source_target_pairs={{0,2},{2,0},{4,6},{6,4},{1,3},{3,1},{5,7},{7,5},{8,10},{10,8},{12,... | collective-permute-start | bytes 884744 | tf_op jit(solution)/shard_map/ppermute | solution.py:28
  444.5 12.1 %collective-permute-start.30 = (bf16[1,192,768]{2,1,0:T(8,128)(2,1)S(1)}, bf16[1,192,768]{2,1,0:T(8,128)(2,1)S(1)}, u32[]{:S(2)}, u32[]{:S(2)}) collective-permute-start(bf16[1,192,768]{2,1,0:T(8,128)(2,1)S(1)} %get-tuple-element.123), channel_id=1, source_target_pairs={{0,16},{8,24},{16,0},{24,8},{1,17},{9,25},{17,1},{25,9},{2,18},{10... | collective-permute-start | bytes 884744 | tf_op jit(solution)/shard_map/ppermute | solution.py:28
  (160 other events, 1203.7 us)
